TPU v7x, 128 devices: a whole 4x4x4 slice. The times are simulated.
128 devices in a mesh: ctx: 32 (over y, x, core), head: 4 (over z).
Axes of the slice: x: 4, y: 4, z: 4, core: 2. Of those that a mesh axis runs over, the one named last changes fastest.
Arguments:
- query_raw: bfloat16 [16384, 2048], P('ctx', 'head'), may hold values from -120 to 120
- key_raw: bfloat16 [16384, 2048], P('ctx', 'head'), may hold values from -120 to 120
- value_raw: bfloat16 [16384, 4096], P('ctx', 'head'), may hold values from -120 to 120
- conv_query: bfloat16 [4, 2048], P(None, 'head'), may hold values from -3 to 3
- conv_key: bfloat16 [4, 2048], P(None, 'head'), may hold values from -3 to 3
- conv_value: bfloat16 [4, 4096], P(None, 'head'), may hold values from -3 to 3
- decay_log: float32 [32, 16384], P('head', 'ctx'), may hold values from -0.6 to 0, as said below
- write_beta: float32 [32, 16384], P('head', 'ctx'), may hold values from 0 to 1
- gate_input: bfloat16 [16384, 4096], P('ctx', 'head'), may hold values from -6 to 6
- norm_gain: float32 [128], replicated, may hold values from 0.5 to 1.5
- out_weight: bfloat16 [4096, 2048], P('head'), may hold values from -0.125 to 0.125
Outputs:
- mixed: bfloat16 [16384, 2048], P('ctx', 'head')
Inputs may be any that keep to these rules, and one draw needn't show every extreme that they name: `decay_log`: natural logarithm of a decay factor.
All inputs are finite; a program needn't handle non-finite values.
Results may differ from a plain program's by a relative error of at most 0.014.
Values may be sent and summed in bfloat16 or wider, within the bound.
No kernel may reach another device: no remote copies, remote signals or barrier semaphores. Data moves between devices by JAX's collectives and lax.ppermute only.
A program may use at most 128 MiB of HBM per device.

v0:
```python
import jax
import jax.numpy as jnp
from jax import lax
from jax.sharding import PartitionSpec as P

DK = 128
DV = 128
CONV = 4
BLOCK = 64


highest = lax.Precision.HIGHEST


def shifted(value, axis, by):
    length = lax.axis_size(axis)
    pairs = [(i, i + by) for i in range(length) if 0 <= i + by < length]
    return lax.ppermute(value, axis, pairs)


def conv_silu(raw_rows, rim_rows, conv_weight):
    widths = conv_weight.shape[0]
    length = raw_rows.shape[0]
    padded = jnp.concatenate([rim_rows.astype(jnp.float32), raw_rows.astype(jnp.float32)], 0)
    weights = conv_weight.astype(jnp.float32)
    running = jnp.zeros((length, raw_rows.shape[1]), jnp.float32)
    for offset in range(widths):
        running = running + weights[offset] * padded[offset : offset + length]
    return jax.nn.silu(running)


def unit_rows(values):
    return values * lax.rsqrt(jnp.sum(values * values, -1, keepdims=True) + 1e-06)


def prepare(key_block, value_block, cumulative, beta_blocks):
    length = key_block.shape[-2]
    inner_keys = jnp.einsum("...id,...jd->...ij", key_block, key_block, precision=highest)
    positions = jnp.arange(length)
    strict_lower = positions[:, None] > positions[None, :]
    causal = positions[:, None] >= positions[None, :]
    spread = jnp.exp(jnp.where(causal, cumulative[..., :, None] - cumulative[..., None, :], 0.0))
    lower_part = jnp.where(strict_lower, beta_blocks[..., :, None] * inner_keys * spread, 0.0)
    system = jnp.eye(length, dtype=jnp.float32) + lower_part
    key_mix = jax.scipy.linalg.solve_triangular(
        system, (beta_blocks * jnp.exp(cumulative))[..., None] * key_block, lower=True
    )
    value_mix = jax.scipy.linalg.solve_triangular(
        system, beta_blocks[..., None] * value_block, lower=True
    )
    return (key_mix, value_mix, spread, causal)


def block_outputs(
    carry_state, query_block, key_block, key_mix, value_mix, cumulative, spread, causal
):
    fresh_values = value_mix - jnp.einsum("hcd,hvd->hcv", key_mix, carry_state, precision=highest)
    scores = jnp.where(
        causal, jnp.einsum("hid,hjd->hij", query_block, key_block, precision=highest) * spread, 0.0
    )
    result = jnp.einsum(
        "hcd,hvd->hcv", query_block * jnp.exp(cumulative)[..., None], carry_state, precision=highest
    )
    result = result + jnp.einsum("hij,hjv->hiv", scores, fresh_values, precision=highest)
    last_cum = cumulative[:, -1]
    carried = jnp.exp(last_cum[:, None] - cumulative)[..., None] * fresh_values
    carry_state = jnp.exp(last_cum)[:, None, None] * carry_state + jnp.einsum(
        "hcv,hcd->hvd", carried, key_block, precision=highest
    )
    return (carry_state, result)


def batch_product(left_side, right_side):
    return jnp.einsum("hab,hbc->hac", left_side, right_side, precision=highest)


def body(
    query_raw,
    key_raw,
    value_raw,
    conv_query,
    conv_key,
    conv_value,
    decay_log,
    write_beta,
    gate_input,
    norm_gain,
    out_weight,
):
    local_tokens = query_raw.shape[0]
    key_heads = query_raw.shape[1] // DK
    value_heads = value_raw.shape[1] // DV
    head_ratio = value_heads // key_heads
    block_count = local_tokens // BLOCK
    margin = CONV - 1
    rim_rows = shifted(
        (
            query_raw[local_tokens - margin :],
            key_raw[local_tokens - margin :],
            value_raw[local_tokens - margin :],
        ),
        "ctx",
        1,
    )
    queries = unit_rows(
        conv_silu(query_raw, rim_rows[0], conv_query).reshape(local_tokens, key_heads, DK)
    ) * DK ** (-0.5)
    key_unit = unit_rows(
        conv_silu(key_raw, rim_rows[1], conv_key).reshape(local_tokens, key_heads, DK)
    )
    values = conv_silu(value_raw, rim_rows[2], conv_value).reshape(local_tokens, value_heads, DV)

    def blocks(array, heads, width):
        return array.reshape(block_count, BLOCK, heads, width).transpose(0, 2, 1, 3)

    query_blocks = jnp.repeat(blocks(queries, key_heads, DK), head_ratio, axis=1)
    key_blocks = jnp.repeat(blocks(key_unit, key_heads, DK), head_ratio, axis=1)
    value_blocks = blocks(values, value_heads, DV)
    cumulative = jnp.cumsum(
        decay_log.reshape(value_heads, block_count, BLOCK).transpose(1, 0, 2), axis=-1
    )
    beta_blocks = write_beta.reshape(value_heads, block_count, BLOCK).transpose(1, 0, 2)
    key_mix, value_mix, spread, causal = prepare(key_blocks, value_blocks, cumulative, beta_blocks)
    identity = jnp.broadcast_to(jnp.eye(DK, dtype=jnp.float32), (value_heads, DK, DK))
    empty_state = jnp.zeros((value_heads, DV, DK), jnp.float32)

    def compose(carry, inputs):
        transit, offset = carry
        key_block, mix_block, value_block, cumul_block = inputs
        last_cum = cumul_block[:, -1]
        tail_weight = jnp.exp(last_cum[:, None] - cumul_block)[..., None]
        step_transit = jnp.exp(last_cum)[:, None, None] * identity - jnp.einsum(
            "hcd,hce->hde", mix_block * tail_weight, key_block, precision=highest
        )
        step_offset = jnp.einsum(
            "hcv,hce->hve", value_block * tail_weight, key_block, precision=highest
        )
        return (
            (
                batch_product(transit, step_transit),
                batch_product(offset, step_transit) + step_offset,
            ),
            None,
        )

    (transit, offset), unused = lax.scan(
        compose, (identity, empty_state), (key_blocks, key_mix, value_mix, cumulative)
    )

    def relay_step(counter, incoming):
        return shifted(
            (batch_product(incoming, transit) + offset).astype(jnp.bfloat16), "ctx", 1
        ).astype(jnp.float32)

    start_state = lax.fori_loop(0, lax.axis_size("ctx") - 1, relay_step, empty_state)

    def advance(carry_state, inputs):
        query_block, key_block, mix_block, value_block, cumul_block, spread_block = inputs
        return block_outputs(
            carry_state,
            query_block,
            key_block,
            mix_block,
            value_block,
            cumul_block,
            spread_block,
            causal,
        )

    final_state, outputs = lax.scan(
        advance, start_state, (query_blocks, key_blocks, key_mix, value_mix, cumulative, spread)
    )
    heads_out = outputs.transpose(0, 2, 1, 3).reshape(local_tokens, value_heads, DV)
    normed = heads_out * lax.rsqrt(jnp.mean(heads_out * heads_out, -1, keepdims=True) + 1e-06)
    gated = (
        normed
        * norm_gain
        * jax.nn.silu(gate_input.astype(jnp.float32).reshape(local_tokens, value_heads, DV))
    )
    hidden = gated.astype(jnp.bfloat16).reshape(local_tokens, value_heads * DV)
    summed = lax.psum_scatter(
        lax.dot_general(
            out_weight, hidden, (((0,), (1,)), ((), ())), preferred_element_type=jnp.float32
        ).astype(jnp.bfloat16),
        "head",
        scatter_dimension=0,
        tiled=True,
    ).astype(jnp.float32)
    return jnp.transpose(summed).astype(jnp.bfloat16)


def solution(mesh):
    return jax.shard_map(
        body,
        mesh=mesh,
        in_specs=(
            P("ctx", "head"),
            P("ctx", "head"),
            P("ctx", "head"),
            P(None, "head"),
            P(None, "head"),
            P(None, "head"),
            P("head", "ctx"),
            P("head", "ctx"),
            P("ctx", "head"),
            P(),
            P("head", None),
        ),
        out_specs=P("ctx", "head"),
        check_vma=False,
    )
```

profile of v0, /device:TPU:32, one launch (start us, length us, event | category | flops | bytes accessed | tf_op | source)
XLA Modules:
  0.0 970.8 jit_solution(11066475534241974338)
XLA Ops:
  39.1 316.0 %custom-call.6 = f32[8,8,1,64,64]{3,4,2,1,0:T(8,128)} custom-call(f32[8,8,1,64,64]{4,3,2,1,0:T(8,128)} %select_bitcast_fusion), custom_call_target="InvertDiagBlocksLowerTriangular" | custom-call | tf_op jit(solution)/shard_map/jit(_solve_triangular)/vmap(vmap())/triangular_solve | solution.py:45
  366.6 7.0 fusion.59
  384.8 80.1 %while.38 = (s32[]{:T(128)}, f32[8,128,128]{1,2,0:T(8,128)}, f32[8,128,128]{1,2,0:T(8,128)}, f32[8,8,64]{2,1,0:T(8,128)S(1)}, f32[8,8,64,128]{3,2,1,0:T(8,128)},...) while((s32[]{:T(128)}, f32[8,128,128]{1,2,0:T(8,128)}, ...), condition=%wide.region_3.5_spmd.clone, body=%wide.region_2.4_spmd.clone.sunk | while | flops 604635648 | bytes 6900511 | solution.py:146
  468.2 348.7 %while.39 = (s32[]{:T(128)}, f32[8,128,128]{2,1,0:T(8,128)S(1)}, f32[8,128,128]{2,1,0:T(8,128)S(1)}, f32[8,128,128]{2,1,0:T(8,128)}, s32[]{:T(128)}, /*index=5*/s32[]{:T(128)}) while((s32[]{:T(128)}, f32[8,128,128]{2,1,0:T(8,128)S(1)}, f32[8,128,128]{2,1,0:T(8,128)S(1)}, f32[8,128,128]{2,1,0:T(8,128)}, s32[]{:T(128)}, ...), condition=%wide.region_5.7_spmd.clone, body=%wide.region_4.6_spmd.clone.sunk | while | flops 201850880 | bytes 3670135 | solution.py:155
  486.0 6.5 collective-permute-start
  610.7 6.5 collective-permute-start
  621.1 6.9 collective-permute-start
  631.9 8.6 collective-permute-start
  644.4 8.7 collective-permute-start
  656.9 8.7 collective-permute-start
  669.4 8.6 collective-permute-start
  681.9 8.7 collective-permute-start
  694.4 8.7 collective-permute-start
  706.9 8.6 collective-permute-start
  719.4 8.7 collective-permute-start
  731.9 8.7 collective-permute-start
  744.4 8.6 collective-permute-start
  756.9 8.7 collective-permute-start
  769.4 8.7 collective-permute-start
  781.9 8.6 collective-permute-start
  794.4 8.7 collective-permute-start
  806.9 8.7 collective-permute-start
  819.8 67.8 %while.37 = (s32[]{:T(128)}, f32[8,128,128]{2,1,0:T(8,128)S(1)}, f32[8,8,64,128]{3,2,1,0:T(8,128)}, f32[8,8,64]{2,1,0:T(8,128)S(1)}, f32[8,8,64,128]{3,2,1,0:T(8...) while((s32[]{:T(128)}, f32[8,128,128]{2,1,0:T(8,128)S(1)}, ...), condition=%wide.region_8.10_spmd.clone, body=%wide.region_7.9_spmd.clone.sunk | while | flops 403247616 | bytes 5799197 | solution.py:170
  897.0 67.0 %reduce-scatter.2.cloned.1.call-done = bf16[512,512]{0,1:T(8,128)(2,1)} async-done(((bf16[2048,512]{0,1:T(8,128)(2,1)}), bf16[512,512]{0,1:T(8,128)(2,1)}) %reduce-scatter.2.cloned.1.call-update) | async-done | bytes 524304 | tf_op jit(solution)/shard_map/reduce_scatter | solution.py:181
  (342 shorter events, 416.0 us)
Async XLA Ops:
  6.5 957.4 %reduce-scatter.2.cloned.1.call-start = ((), (), s32[]{:S(2)}) async-start(), calls=%async_computation.1 | async-start | bytes 2621440 | tf_op jit(solution)/shard_map/reduce_scatter | solution.py:181
  7.3 19.5 %collective-permute-start.1 = (bf16[3,512]{1,0:T(4,128)(2,1)S(1)}, bf16[3,512]{1,0:T(4,128)(2,1)S(1)}, u32[]{:S(2)}, u32[]{:S(2)}) collective-permute-start(bf16[3,512]{1,0:T(4,128)(2,1)S(1)} %slice.83), channel_id=1, source_target_pairs={{0,4},{4,8},{8,12},{12,16},{16,20},{20,24},{24,28},{28,32},{32,36}... | collective-permute-start | bytes 9224 | tf_op jit(solution)/shard_map/ppermute | solution.py:18
  9.8 365.7 %collective-permute-start.2 = (bf16[3,1024]{1,0:T(4,128)(2,1)S(1)}, bf16[3,1024]{1,0:T(4,128)(2,1)S(1)}, u32[]{:S(2)}, u32[]{:S(2)}) collective-permute-start(bf16[3,1024]{1,0:T(4,128)(2,1)S(1)} %slice.91), channel_id=1, source_target_pairs={{0,4},{4,8},{8,12},{12,16},{16,20},{20,24},{24,28},{28,32},{32,36}... | collective-permute-start | bytes 18440 | tf_op jit(solution)/shard_map/ppermute | solution.py:18
  14.2 340.9 %collective-permute-start.3 = (bf16[3,512]{1,0:T(4,128)(2,1)S(1)}, bf16[3,512]{1,0:T(4,128)(2,1)S(1)}, u32[]{:S(2)}, u32[]{:S(2)}) collective-permute-start(bf16[3,512]{1,0:T(4,128)(2,1)S(1)} %slice.99), channel_id=1, source_target_pairs={{0,4},{4,8},{8,12},{12,16},{16,20},{20,24},{24,28},{28,32},{32,36}... | collective-permute-start | bytes 9224 | tf_op jit(solution)/shard_map/ppermute | solution.py:18
  486.0 7.9 collective-permute-start
  496.4 7.9 collective-permute-start
  548.4 7.9 collective-permute-start
  610.7 7.9 collective-permute-start
  621.1 8.3 collective-permute-start
  631.9 10.0 %collective-permute-start = (bf16[8,128,128]{2,1,0:T(8,128)(2,1)}, bf16[8,128,128]{2,1,0:T(8,128)(2,1)S(1)}, u32[]{:S(2)}, u32[]{:S(2)}) collective-permute-start(bf16[8,128,128]{2,1,0:T(8,128)(2,1)} %fusion.148), channel_id=1, source_target_pairs={{0,4},{4,8},{8,12},{12,16},{16,20},{20,24},{24,28},{28,32},{32,36}... | collective-permute-start | bytes 786440 | tf_op jit(solution)/shard_map/while/body/eval_jaxpr/ppermute | solution.py:18
  644.4 10.0 %collective-permute-start = (bf16[8,128,128]{2,1,0:T(8,128)(2,1)}, bf16[8,128,128]{2,1,0:T(8,128)(2,1)S(1)}, u32[]{:S(2)}, u32[]{:S(2)}) collective-permute-start(bf16[8,128,128]{2,1,0:T(8,128)(2,1)} %fusion.148), channel_id=1, source_target_pairs={{0,4},{4,8},{8,12},{12,16},{16,20},{20,24},{24,28},{28,32},{32,36}... | collective-permute-start | bytes 786440 | tf_op jit(solution)/shard_map/while/body/eval_jaxpr/ppermute | solution.py:18
  656.9 10.0 %collective-permute-start = (bf16[8,128,128]{2,1,0:T(8,128)(2,1)}, bf16[8,128,128]{2,1,0:T(8,128)(2,1)S(1)}, u32[]{:S(2)}, u32[]{:S(2)}) collective-permute-start(bf16[8,128,128]{2,1,0:T(8,128)(2,1)} %fusion.148), channel_id=1, source_target_pairs={{0,4},{4,8},{8,12},{12,16},{16,20},{20,24},{24,28},{28,32},{32,36}... | collective-permute-start | bytes 786440 | tf_op jit(solution)/shard_map/while/body/eval_jaxpr/ppermute | solution.py:18
  669.4 10.0 %collective-permute-start = (bf16[8,128,128]{2,1,0:T(8,128)(2,1)}, bf16[8,128,128]{2,1,0:T(8,128)(2,1)S(1)}, u32[]{:S(2)}, u32[]{:S(2)}) collective-permute-start(bf16[8,128,128]{2,1,0:T(8,128)(2,1)} %fusion.148), channel_id=1, source_target_pairs={{0,4},{4,8},{8,12},{12,16},{16,20},{20,24},{24,28},{28,32},{32,36}... | collective-permute-start | bytes 786440 | tf_op jit(solution)/shard_map/while/body/eval_jaxpr/ppermute | solution.py:18
  681.9 10.0 %collective-permute-start = (bf16[8,128,128]{2,1,0:T(8,128)(2,1)}, bf16[8,128,128]{2,1,0:T(8,128)(2,1)S(1)}, u32[]{:S(2)}, u32[]{:S(2)}) collective-permute-start(bf16[8,128,128]{2,1,0:T(8,128)(2,1)} %fusion.148), channel_id=1, source_target_pairs={{0,4},{4,8},{8,12},{12,16},{16,20},{20,24},{24,28},{28,32},{32,36}... | collective-permute-start | bytes 786440 | tf_op jit(solution)/shard_map/while/body/eval_jaxpr/ppermute | solution.py:18
  694.4 10.0 %collective-permute-start = (bf16[8,128,128]{2,1,0:T(8,128)(2,1)}, bf16[8,128,128]{2,1,0:T(8,128)(2,1)S(1)}, u32[]{:S(2)}, u32[]{:S(2)}) collective-permute-start(bf16[8,128,128]{2,1,0:T(8,128)(2,1)} %fusion.148), channel_id=1, source_target_pairs={{0,4},{4,8},{8,12},{12,16},{16,20},{20,24},{24,28},{28,32},{32,36}... | collective-permute-start | bytes 786440 | tf_op jit(solution)/shard_map/while/body/eval_jaxpr/ppermute | solution.py:18
  706.9 10.0 %collective-permute-start = (bf16[8,128,128]{2,1,0:T(8,128)(2,1)}, bf16[8,128,128]{2,1,0:T(8,128)(2,1)S(1)}, u32[]{:S(2)}, u32[]{:S(2)}) collective-permute-start(bf16[8,128,128]{2,1,0:T(8,128)(2,1)} %fusion.148), channel_id=1, source_target_pairs={{0,4},{4,8},{8,12},{12,16},{16,20},{20,24},{24,28},{28,32},{32,36}... | collective-permute-start | bytes 786440 | tf_op jit(solution)/shard_map/while/body/eval_jaxpr/ppermute | solution.py:18
  719.4 10.0 %collective-permute-start = (bf16[8,128,128]{2,1,0:T(8,128)(2,1)}, bf16[8,128,128]{2,1,0:T(8,128)(2,1)S(1)}, u32[]{:S(2)}, u32[]{:S(2)}) collective-permute-start(bf16[8,128,128]{2,1,0:T(8,128)(2,1)} %fusion.148), channel_id=1, source_target_pairs={{0,4},{4,8},{8,12},{12,16},{16,20},{20,24},{24,28},{28,32},{32,36}... | collective-permute-start | bytes 786440 | tf_op jit(solution)/shard_map/while/body/eval_jaxpr/ppermute | solution.py:18
  731.9 10.0 %collective-permute-start = (bf16[8,128,128]{2,1,0:T(8,128)(2,1)}, bf16[8,128,128]{2,1,0:T(8,128)(2,1)S(1)}, u32[]{:S(2)}, u32[]{:S(2)}) collective-permute-start(bf16[8,128,128]{2,1,0:T(8,128)(2,1)} %fusion.148), channel_id=1, source_target_pairs={{0,4},{4,8},{8,12},{12,16},{16,20},{20,24},{24,28},{28,32},{32,36}... | collective-permute-start | bytes 786440 | tf_op jit(solution)/shard_map/while/body/eval_jaxpr/ppermute | solution.py:18
  744.4 10.0 %collective-permute-start = (bf16[8,128,128]{2,1,0:T(8,128)(2,1)}, bf16[8,128,128]{2,1,0:T(8,128)(2,1)S(1)}, u32[]{:S(2)}, u32[]{:S(2)}) collective-permute-start(bf16[8,128,128]{2,1,0:T(8,128)(2,1)} %fusion.148), channel_id=1, source_target_pairs={{0,4},{4,8},{8,12},{12,16},{16,20},{20,24},{24,28},{28,32},{32,36}... | collective-permute-start | bytes 786440 | tf_op jit(solution)/shard_map/while/body/eval_jaxpr/ppermute | solution.py:18
  756.9 10.0 %collective-permute-start = (bf16[8,128,128]{2,1,0:T(8,128)(2,1)}, bf16[8,128,128]{2,1,0:T(8,128)(2,1)S(1)}, u32[]{:S(2)}, u32[]{:S(2)}) collective-permute-start(bf16[8,128,128]{2,1,0:T(8,128)(2,1)} %fusion.148), channel_id=1, source_target_pairs={{0,4},{4,8},{8,12},{12,16},{16,20},{20,24},{24,28},{28,32},{32,36}... | collective-permute-start | bytes 786440 | tf_op jit(solution)/shard_map/while/body/eval_jaxpr/ppermute | solution.py:18
  769.4 10.0 %collective-permute-start = (bf16[8,128,128]{2,1,0:T(8,128)(2,1)}, bf16[8,128,128]{2,1,0:T(8,128)(2,1)S(1)}, u32[]{:S(2)}, u32[]{:S(2)}) collective-permute-start(bf16[8,128,128]{2,1,0:T(8,128)(2,1)} %fusion.148), channel_id=1, source_target_pairs={{0,4},{4,8},{8,12},{12,16},{16,20},{20,24},{24,28},{28,32},{32,36}... | collective-permute-start | bytes 786440 | tf_op jit(solution)/shard_map/while/body/eval_jaxpr/ppermute | solution.py:18
  781.9 10.0 %collective-permute-start = (bf16[8,128,128]{2,1,0:T(8,128)(2,1)}, bf16[8,128,128]{2,1,0:T(8,128)(2,1)S(1)}, u32[]{:S(2)}, u32[]{:S(2)}) collective-permute-start(bf16[8,128,128]{2,1,0:T(8,128)(2,1)} %fusion.148), channel_id=1, source_target_pairs={{0,4},{4,8},{8,12},{12,16},{16,20},{20,24},{24,28},{28,32},{32,36}... | collective-permute-start | bytes 786440 | tf_op jit(solution)/shard_map/while/body/eval_jaxpr/ppermute | solution.py:18
  794.4 10.0 %collective-permute-start = (bf16[8,128,128]{2,1,0:T(8,128)(2,1)}, bf16[8,128,128]{2,1,0:T(8,128)(2,1)S(1)}, u32[]{:S(2)}, u32[]{:S(2)}) collective-permute-start(bf16[8,128,128]{2,1,0:T(8,128)(2,1)} %fusion.148), channel_id=1, source_target_pairs={{0,4},{4,8},{8,12},{12,16},{16,20},{20,24},{24,28},{28,32},{32,36}... | collective-permute-start | bytes 786440 | tf_op jit(solution)/shard_map/while/body/eval_jaxpr/ppermute | solution.py:18
  806.9 10.0 %collective-permute-start = (bf16[8,128,128]{2,1,0:T(8,128)(2,1)}, bf16[8,128,128]{2,1,0:T(8,128)(2,1)S(1)}, u32[]{:S(2)}, u32[]{:S(2)}) collective-permute-start(bf16[8,128,128]{2,1,0:T(8,128)(2,1)} %fusion.148), channel_id=1, source_target_pairs={{0,4},{4,8},{8,12},{12,16},{16,20},{20,24},{24,28},{28,32},{32,36}... | collective-permute-start | bytes 786440 | tf_op jit(solution)/shard_map/while/body/eval_jaxpr/ppermute | solution.py:18
  (21 other events, 141.4 us)
Sparse Core Ops, SparseCore 0:
  897.1 66.8 reduce-scatter.1
where the time goes:
time: 978 us; the launch traced here: 971 us
  other arithmetic  340 us (35%)
  starting transfers between devices  237 us (24%)
  matrix products  232 us (24%)
  waiting for transfers between devices  109 us (11%)
  local copies, waits for them, and re-layouts  38.7 us (4%)
  between operations  13.7 us (1%)
    another operation x2, other arithmetic, prepare(): jax.scipy.linalg.solve_triangular(system, (beta_blocks * jnp.exp(cumulati...  316 us
    ppermute x34, starting transfers between devices, shifted(): return lax.ppermute(value, axis, pairs)  237 us
    dot_general x47, matrix products, batch_product(): return jnp.einsum('hab,hbc->hac', left_side, right_side, precision=highest)  106 us
    reduce_scatter x1, waiting for transfers between devices, body(): lax.psum_scatter(lax.dot_general(out_weight, hidden, (((0,), (1,)), ((),...  67 us
    ppermute x34, waiting for transfers between devices, shifted(): return lax.ppermute(value, axis, pairs)  41.5 us
    dot_general x8, matrix products, compose(): jnp.einsum('hcv,hce->hve', value_block * tail_weight, key_block, precisio...  22.6 us
  transfers between devices with their start and end apart: 35, of which 32 were waited for; matrix products, arithmetic and copies ran while one was open for 37% of the time, Pallas kernels for 0%

commit v1 on v0

v1 whole, which is shorter than its diff:
```python
import jax
import jax.numpy as jnp
from jax import lax
from jax.experimental import pallas as pl
from jax.experimental.pallas import tpu as pltpu
from jax.sharding import PartitionSpec as P

DK = 128
DV = 128
CHUNK = 128
ROW = 8
EXTRA = 16
VMEM_BYTES = 56 * 1024 * 1024

f32 = jnp.float32
bf16 = jnp.bfloat16
highest = lax.Precision.HIGHEST


def mm(a, b, dims=((1,), (0,))):
    return lax.dot_general(a, b, (dims, ((), ())), preferred_element_type=f32)


def mm_exact(a, b, dims=((1,), (0,))):
    return lax.dot_general(a, b, (dims, ((), ())), preferred_element_type=f32, precision=highest)


NT = ((1,), (1,))
TN = ((0,), (0,))


def silu(x):
    return x / (1.0 + jnp.exp(-x))


def split3(x):
    hi = x.astype(bf16)
    rest = x - hi.astype(f32)
    mid = rest.astype(bf16)
    low = (rest - mid.astype(f32)).astype(bf16)
    return hi, mid, low


def prep_kernel(
    q_ref, k_ref, v_ref, rim_ref, cq_ref, ck_ref, cv_ref, dl_ref, wb_ref,
    o_ref, qe_ref, x_ref,
    pad, ks, qs, vs, lm, tm, rm, am, zt, gs,
):
    tokens, qw = q_ref.shape
    vw = v_ref.shape[1]
    key_heads = qw // DK
    heads = vw // DV
    ratio = heads // key_heads
    c = CHUNK
    ii = lax.broadcasted_iota(jnp.int32, (c, c), 0)
    jj = lax.broadcasted_iota(jnp.int32, (c, c), 1)
    xor = jnp.where(ii >= jj, ii ^ jj, -1)
    lower = (ii >= jj).astype(f32)
    upper = (ii <= jj).astype(f32)
    eye = (ii == jj).astype(f32)
    wq = cq_ref[...].astype(f32)
    wk = ck_ref[...].astype(f32)
    wv = cv_ref[...].astype(f32)
    pad[0:8, :] = rim_ref[...].astype(f32)
    zt[...] = jnp.zeros_like(zt)
    gs[...] = jnp.zeros_like(gs)

    def conv(col, w, wcol):
        acc = w[0:1, wcol : wcol + 128] * pad[5 : 5 + c, col : col + 128]
        for j in range(1, 4):
            acc = acc + w[j : j + 1, wcol : wcol + 128] * pad[5 + j : 5 + j + c, col : col + 128]
        return silu(acc)

    def unit(x):
        return x * lax.rsqrt(jnp.sum(x * x, -1, keepdims=True) + 1e-06)

    def chunk(b, unused):
        base = pl.multiple_of(b * c, c)
        rows = pl.ds(base, c)
        pad[8 : 8 + c, 0:qw] = q_ref[rows, :].astype(f32)
        pad[8 : 8 + c, qw : 2 * qw] = k_ref[rows, :].astype(f32)
        pad[8 : 8 + c, 2 * qw : 2 * qw + vw] = v_ref[rows, :].astype(f32)
        for h in range(key_heads):
            qs[h] = unit(conv(h * DK, wq, h * DK)) * DK ** (-0.5)
            ks[h] = unit(conv(qw + h * DK, wk, h * DK))
        for h in range(heads):
            vs[h] = conv(2 * qw + h * DV, wv, h * DV)
        pad[0:8, :] = pad[c : c + 8, :]

        dl = dl_ref[:, rows]
        wb = wb_ref[:, rows]
        c_row = mm_exact(dl, upper)
        c_col = mm_exact(lower, dl, NT)
        b_col = mm_exact(eye, wb, NT)
        last = c_col[c - 1 : c, :]
        ec = jnp.exp(c_col)
        be = b_col * ec
        tail = jnp.exp(last - c_col)
        g0 = gs[0:1, 0:heads]
        gam = jnp.broadcast_to(jnp.exp(g0), (c, heads))
        eg = jnp.exp(c_col + g0)
        el = jnp.broadcast_to(jnp.exp(last), (c, heads))
        gs[0:1, 0:heads] = g0 + last

        for kh in range(key_heads):
            kb = ks[kh].astype(bf16)
            qb = qs[kh].astype(bf16)
            gram = mm(kb, kb, NT)
            qk = mm(qb, kb, NT)
            for r in range(ratio):
                h = kh * ratio + r
                diff = c_col[:, h : h + 1] - c_row[h : h + 1, :]
                spread = jnp.exp(jnp.where(xor >= 0, diff, -1e30))
                low = b_col[:, h : h + 1] * gram * spread
                lm[h] = low
                am[h] = (qk * spread).astype(bf16)
                tm[h] = (eye - jnp.where(xor == 1, low, 0.0)).astype(bf16)
        s = 2
        while s < c:
            pick = (xor >= s) & (xor < 2 * s)
            for h in range(heads):
                rm[h] = mm(jnp.where(pick, lm[h], 0.0).astype(bf16), tm[h]).astype(bf16)
            for h in range(heads):
                tm[h] = tm[h] - mm(tm[h], rm[h]).astype(bf16)
            s *= 2
        for h in range(heads):
            kh = h // ratio
            k = ks[kh]
            q = qs[kh]
            rhs = jnp.concatenate([b_col[:, h : h + 1] * vs[h], be[:, h : h + 1] * k], 1).astype(bf16)
            uw = mm(tm[h], rhs)
            w = uw[:, DV:]
            z = zt[h]
            zb = z.astype(bf16)
            fresh = jnp.concatenate([uw[:, :DV], gam[:, h : h + 1] * w], 1) - mm(w.astype(bf16), zb)
            out = mm((ec[:, h : h + 1] * q).astype(bf16), zb) + mm(am[h], fresh.astype(bf16))
            o_ref[rows, h * DV : (h + 1) * DV] = out[:, :DV]
            qe_ref[rows, h * DK : (h + 1) * DK] = (eg[:, h : h + 1] * q - out[:, DV:]).astype(bf16)
            zt[h] = el[:, h : h + 1] * z + mm(
                k.astype(bf16), (tail[:, h : h + 1] * fresh).astype(bf16), TN
            )
        return unused

    lax.fori_loop(0, tokens // c, chunk, 0)
    total = jnp.broadcast_to(gs[0:1, 0:heads], (EXTRA, heads))
    row = lax.broadcasted_iota(jnp.int32, (EXTRA, DV), 0)
    for h in range(heads):
        z = zt[h]
        x_ref[h, 0:DK, :] = z[:, :DV].astype(bf16)
        x_ref[h, DK : 2 * DK, :] = z[:, DV:].astype(bf16)
        full = jnp.broadcast_to(total[:, h : h + 1], (EXTRA, DV))
        hi, mid, low = split3(full)
        x_ref[h, 2 * DK : 2 * DK + EXTRA, :] = jnp.where(
            row == 0, hi.astype(f32), jnp.where(row == 1, mid.astype(f32), jnp.where(row == 2, low.astype(f32), 0.0))
        ).astype(bf16)


def prep(q, k, v, rim, cq, ck, cv, dl, wb):
    tokens, qw = q.shape
    vw = v.shape[1]
    kh, h = qw // DK, vw // DV
    c = CHUNK
    return pl.pallas_call(
        prep_kernel,
        out_shape=(
            jax.ShapeDtypeStruct((tokens, vw), f32),
            jax.ShapeDtypeStruct((tokens, h * DK), bf16),
            jax.ShapeDtypeStruct((h, 2 * DK + EXTRA, DV), bf16),
        ),
        scratch_shapes=[
            pltpu.VMEM((c + 8, 2 * qw + vw), f32),
            pltpu.VMEM((kh, c, DK), f32),
            pltpu.VMEM((kh, c, DK), f32),
            pltpu.VMEM((h, c, DV), f32),
            pltpu.VMEM((h, c, c), f32),
            pltpu.VMEM((h, c, c), bf16),
            pltpu.VMEM((h, c, c), bf16),
            pltpu.VMEM((h, c, c), bf16),
            pltpu.VMEM((h, DK, DV + DK), f32),
            pltpu.VMEM((8, 128), f32),
        ],
        compiler_params=pltpu.CompilerParams(vmem_limit_bytes=VMEM_BYTES),
        name="prep",
    )(q, k, v, rim, cq, ck, cv, dl, wb)


def log_decay(ref, at):
    rows = ref[at, 2 * DK : 2 * DK + EXTRA, :].astype(f32)
    return rows[0:1, :] + rows[1:2, :] + rows[2:3, :]


def row_kernel(x_ref, pre_ref, g_ref, out_ref):
    count = x_ref.shape[0]
    z = jnp.zeros((DK, DV + DK), f32)
    g = jnp.zeros((1, DV), f32)
    for i in range(count):
        pre_ref[i] = z
        g_ref[i] = jnp.broadcast_to(g, (8, DV))
        step = log_decay(x_ref, i)
        d = x_ref[i, DK : 2 * DK, :]
        scale = jnp.broadcast_to(jnp.exp(step), (DK, DV))
        past = jnp.broadcast_to(jnp.exp(g), (DK, DV))
        add = jnp.concatenate([x_ref[i, 0:DK, :].astype(f32), past * d.astype(f32)], 1)
        z = jnp.concatenate([scale, scale], 1) * z - mm(d, z.astype(bf16)) + add
        g = g + step
    out_ref[0:DK, :] = z[:, :DV].astype(bf16)
    out_ref[DK : 2 * DK, :] = z[:, DV:].astype(bf16)
    row = lax.broadcasted_iota(jnp.int32, (EXTRA, DV), 0)
    hi, mid, low = split3(jnp.broadcast_to(g, (EXTRA, DV)))
    out_ref[2 * DK : 2 * DK + EXTRA, :] = jnp.where(
        row == 0, hi.astype(f32), jnp.where(row == 1, mid.astype(f32), jnp.where(row == 2, low.astype(f32), 0.0))
    ).astype(bf16)


def row_prefix(x):
    count = x.shape[0]
    return pl.pallas_call(
        row_kernel,
        out_shape=(
            jax.ShapeDtypeStruct((count, DK, DV + DK), f32),
            jax.ShapeDtypeStruct((count, 8, DV), f32),
            jax.ShapeDtypeStruct((2 * DK + EXTRA, DV), bf16),
        ),
        name="row_prefix",
    )(x)


def start_kernel(y_ref, a_ref, b_ref, c_ref, pre_ref, g_ref, out_ref):
    count = pre_ref.shape[0]
    s = jnp.zeros((DK, DV), f32)
    y = y_ref[0]
    for back, ref in ((3, a_ref), (2, b_ref), (1, c_ref)):
        rows = ref[2 * DK : 2 * DK + EXTRA, :].astype(f32)
        step = rows[0:1, :] + rows[1:2, :] + rows[2:3, :]
        scale = jnp.broadcast_to(jnp.exp(step), (DK, DV))
        after = scale * s - mm(ref[DK : 2 * DK, :], s.astype(bf16)) + ref[0:DK, :].astype(f32)
        s = jnp.where(y >= back, after, s)
    sb = s.astype(bf16)
    for i in range(count):
        z = pre_ref[i]
        scale = jnp.broadcast_to(jnp.exp(g_ref[i, 0:1, :]), (DK, DV))
        out_ref[i] = (scale * s - mm(z[:, DV:].astype(bf16), sb) + z[:, :DV]).astype(bf16)


def start_states(y, a, b, c, pre, g):
    count = pre.shape[0]
    return pl.pallas_call(
        start_kernel,
        in_specs=[pl.BlockSpec(memory_space=pltpu.SMEM)] + [pl.BlockSpec(memory_space=pltpu.VMEM)] * 5,
        out_shape=jax.ShapeDtypeStruct((count, DK, DV), bf16),
        name="start_states",
    )(y, a, b, c, pre, g)


def hidden_kernel(col_ref, o_ref, qe_ref, s_ref, gate_ref, gain_ref, w_ref, hid_ref, p_ref):
    heads = s_ref.shape[0]
    tokens = o_ref.shape[0]
    gain = gain_ref[...]
    for h in range(heads):
        cols = slice(h * DV, (h + 1) * DV)
        x = o_ref[:, cols] + mm(qe_ref[:, cols], s_ref[h])
        x = x * lax.rsqrt(jnp.mean(x * x, -1, keepdims=True) + 1e-06)
        hid_ref[:, cols] = (x * gain * silu(gate_ref[:, cols].astype(f32))).astype(bf16)
    p_ref[...] = mm(hid_ref[...], w_ref[...]).astype(bf16)


def hidden_part(col, o, qe, s, gate, gain, w):
    tokens, vw = o.shape
    width = w.shape[1] // 4
    full = lambda shape: pl.BlockSpec(shape, lambda i, c: (0,) * len(shape))
    return pl.pallas_call(
        hidden_kernel,
        grid_spec=pltpu.PrefetchScalarGridSpec(
            num_scalar_prefetch=1,
            grid=(1,),
            in_specs=[
                full(o.shape), full(qe.shape), full(s.shape), full(gate.shape), full(gain.shape),
                pl.BlockSpec((vw, width), lambda i, c: (0, c[0])),
            ],
            out_specs=[full((tokens, vw)), full((tokens, width))],
        ),
        out_shape=(
            jax.ShapeDtypeStruct((tokens, vw), bf16),
            jax.ShapeDtypeStruct((tokens, width), bf16),
        ),
        compiler_params=pltpu.CompilerParams(vmem_limit_bytes=VMEM_BYTES),
        name="hidden_part",
    )(col, o, qe, s, gate, gain, w)


def part_kernel(col_ref, hid_ref, w_ref, p_ref):
    p_ref[...] = mm(hid_ref[...], w_ref[...]).astype(bf16)


def part(col, hid, w):
    tokens, vw = hid.shape
    width = w.shape[1] // 4
    return pl.pallas_call(
        part_kernel,
        grid_spec=pltpu.PrefetchScalarGridSpec(
            num_scalar_prefetch=1,
            grid=(1,),
            in_specs=[
                pl.BlockSpec((tokens, vw), lambda i, c: (0, 0)),
                pl.BlockSpec((vw, width), lambda i, c: (0, c[0])),
            ],
            out_specs=pl.BlockSpec((tokens, width), lambda i, c: (0, 0)),
        ),
        out_shape=jax.ShapeDtypeStruct((tokens, width), bf16),
        compiler_params=pltpu.CompilerParams(vmem_limit_bytes=VMEM_BYTES),
        name="part",
    )(col, hid, w)


def body(q, k, v, cq, ck, cv, decay_log, write_beta, gate, gain, out_weight):
    tokens = q.shape[0]
    ctx = lax.axis_size("ctx")
    rows = ctx // ROW
    idx = lax.axis_index("ctx")
    z = lax.axis_index("head")
    tails = jnp.concatenate([q[tokens - 8 :], k[tokens - 8 :], v[tokens - 8 :]], 1)
    rim = lax.ppermute(tails, "ctx", [(i, i + 1) for i in range(ctx - 1)])
    o, qe, x = prep(q, k, v, rim, cq, ck, cv, decay_log, write_beta)
    groups = [[y * ROW + j for j in range(ROW)] for y in range(rows)]
    mine = lax.all_to_all(x, "ctx", 0, 0, axis_index_groups=groups, tiled=True)
    pre, g, whole = row_prefix(mine)

    def from_back(d):
        return lax.ppermute(whole, "ctx", [(i, (i + d * ROW) % ctx) for i in range(ctx)])

    s_mine = start_states((idx // ROW).reshape(1), from_back(3), from_back(2), from_back(1), pre, g)
    s = lax.all_to_all(s_mine, "ctx", 0, 0, axis_index_groups=groups, tiled=True)
    col = lambda d: ((z + d) % 4).reshape(1)
    ring = lambda d: [(i, (i + d) % 4) for i in range(4)]
    hid, p2 = hidden_part(col(2), o, qe, s, gate, gain.reshape(1, DV), out_weight)
    r2 = lax.ppermute(p2, "head", ring(2))
    r1 = lax.ppermute(part(col(1), hid, out_weight), "head", ring(1))
    r3 = lax.ppermute(part(col(3), hid, out_weight), "head", ring(3))
    p0 = part(col(0), hid, out_weight)
    total = p0.astype(f32) + r1.astype(f32) + r2.astype(f32) + r3.astype(f32)
    return total.astype(bf16)


def solution(mesh):
    return jax.shard_map(
        body,
        mesh=mesh,
        in_specs=(
            P("ctx", "head"), P("ctx", "head"), P("ctx", "head"),
            P(None, "head"), P(None, "head"), P(None, "head"),
            P("head", "ctx"), P("head", "ctx"), P("ctx", "head"), P(), P("head", None),
        ),
        out_specs=P("ctx", "head"),
        check_vma=False,
    )
```

time: 978 us -> 122 us (0.12)
  other arithmetic: 340 us -> 2.11 us
  matrix products: 232 us -> 0 us
  starting transfers between devices: 237 us -> 16.6 us
  waiting for transfers between devices: 109 us -> 33 us
  Pallas kernels: 0 us -> 47.6 us
  local copies, waits for them, and re-layouts: 38.7 us -> 4.06 us
  blocking collectives: 0 us -> 17.8 us
  between operations: 13.7 us -> 0.07 us
    another operation x3 -> x0, other arithmetic: 318 us -> none  [the longest x2 316 us: prepare(): jax.scipy.linalg.solve_triangular(system, (beta_blocks * jnp.exp(cumulati...]
    ppermute x34 -> x7, starting transfers between devices: 237 us -> 13.2 us  [the longest x3 6.49 us: from_back(): lax.ppermute(whole, 'ctx', [(i, (i + d * ROW) % ctx) for i in range(ctx)])]
    dot_general x105 -> x0, matrix products: 219 us -> none  [the longest x47 106 us: batch_product(): return jnp.einsum('hab,hbc->hac', left_side, right_side, precision=highest)]
    reduce_scatter x1 -> x0, waiting for transfers between devices: 67 us -> none  [body(): lax.psum_scatter(lax.dot_general(out_weight, hidden, (((0,), (1,)), ((),...]
    pallas_call x0 -> x7, Pallas kernels: none -> 47.6 us  [the longest x1 27.7 us: prep(): pl.pallas_call(prep_kernel, out_shape=(jax.ShapeDtypeStruct((tokens, vw),...]
    all_to_all x0 -> x1, blocking collectives: none -> 17.8 us  [body(): mine = lax.all_to_all(x, 'ctx', 0, 0, axis_index_groups=groups, tiled=True)]
    ppermute x34 -> x7, waiting for transfers between devices: 41.5 us -> 25.6 us  [the longest x1 13.2 us: body(): r1 = lax.ppermute(part(col(1), hid, out_weight), 'head', ring(1))]
    another operation x2 -> x0, matrix products: 12.4 us -> none  [the longest x1 7.02 us: prepare(): jax.scipy.linalg.solve_triangular(system, (beta_blocks * jnp.exp(cumulati...]
  transfers between devices with their start and end apart: 35 -> 8, of which waited for: 32 -> 7; matrix products, arithmetic and copies ran while one was open for 37% -> 0% of each run, Pallas kernels for 0% -> 5%
where the time goes in v1:
time: 122 us; the launch traced here: 121 us
  Pallas kernels  47.6 us (39%)
  waiting for transfers between devices  33 us (27%)
  blocking collectives  17.8 us (15%)
  starting transfers between devices  16.6 us (14%)
  local copies, waits for them, and re-layouts  4.06 us (3%)
  other arithmetic  2.11 us (2%)
    pallas_call x1, Pallas kernels, prep(): pl.pallas_call(prep_kernel, out_shape=(jax.ShapeDtypeStruct((tokens, vw),...  27.7 us
    all_to_all x1, blocking collectives, body(): mine = lax.all_to_all(x, 'ctx', 0, 0, axis_index_groups=groups, tiled=True)  17.8 us
    ppermute x1, waiting for transfers between devices, body(): r1 = lax.ppermute(part(col(1), hid, out_weight), 'head', ring(1))  13.2 us
    pallas_call x3, Pallas kernels, part(): pl.pallas_call(part_kernel, grid_spec=pltpu.PrefetchScalarGridSpec(num_sc...  9.13 us
    all_to_all x1, waiting for transfers between devices, body(): lax.all_to_all(s_mine, 'ctx', 0, 0, axis_index_groups=groups, tiled=True)  7.4 us
    ppermute x3, starting transfers between devices, from_back(): lax.ppermute(whole, 'ctx', [(i, (i + d * ROW) % ctx) for i in range(ctx)])  6.49 us
    ppermute x1, waiting for transfers between devices, body(): r2 = lax.ppermute(p2, 'head', ring(2))  6.16 us
    ppermute x3, waiting for transfers between devices, from_back(): lax.ppermute(whole, 'ctx', [(i, (i + d * ROW) % ctx) for i in range(ctx)])  5.34 us
  transfers between devices with their start and end apart: 8, of which 7 were waited for; matrix products, arithmetic and copies ran while one was open for 0% of the time, Pallas kernels for 5%

profile of v1, /device:TPU:32, one launch (start us, length us, event | category | flops | bytes accessed | tf_op | source)
XLA Modules:
  0.0 121.2 jit_solution(7832882643257673416)
XLA Ops:
  0.0 0.7 slice.11
  2.1 1.7 %collective-permute-start = (bf16[8,2048]{1,0:T(8,128)(2,1)S(1)}, bf16[8,2048]{1,0:T(8,128)(2,1)S(1)}, u32[]{:S(2)}, u32[]{:S(2)}) collective-permute-start(bf16[8,2048]{1,0:T(8,128)(2,1)S(1)} %pad_maximum_fusion), channel_id=1, source_target_pairs={{0,4},{4,8},{8,12},{12,16},{16,20},{20,24},{24,28},{28,32},{32,36}... | collective-permute-start | bytes 98312 | tf_op jit(solution)/shard_map/ppermute | solution.py:322
  3.9 0.8 collective-permute-done.rim_ref
  5.3 27.7 %prep.1 = (f32[512,1024]{1,0:T(8,128)}, bf16[512,1024]{1,0:T(8,128)(2,1)}, bf16[8,272,128]{2,1,0:T(8,128)(2,1)}) custom-call(bf16[512,512]{1,0:T(8,128)(2,1)} %q_ref.1, bf16[512,512]{1,0:T(8,128)(2,1)} %k_ref.1, bf16[512,1024]{1,0:T(8,128)(2,1)} %v_ref.1, bf16[8,2048]{1,0:T(8,128)(2,1)} %copy-done.4, bf16[4,512]{1,0:T(4,128)(2,1)} %cq_ref.1, ...), custom_call_target="tpu_custom_call" | custom-call | tf_op jit(solution)/shard_map/prep/pallas_call | solution.py:163
  33.0 17.8 %all_to_all.10.x_ref = bf16[8,272,128]{2,1,0:T(8,128)(2,1)} all-to-all(bf16[8,272,128]{2,1,0:T(8,128)(2,1)} %get-tuple-element.15), channel_id=1, replica_groups={{0,4,8,12,16,20,24,28},{32,36,40,44,48,52,56,60},{64,68,72,76,80,84,88,..., dimensions={0} | all-to-all | bytes 1114112 | tf_op jit(solution)/shard_map/all_to_all | solution.py:325
  50.7 3.1 %row_prefix.1 = (f32[8,128,256]{2,1,0:T(8,128)}, f32[8,8,128]{2,1,0:T(8,128)}, bf16[272,128]{1,0:T(8,128)(2,1)}) custom-call(bf16[8,272,128]{2,1,0:T(8,128)(2,1)} %all_to_all.10.x_ref), custom_call_target="tpu_custom_call" | custom-call | tf_op jit(solution)/shard_map/row_prefix/pallas_call | solution.py:217
  53.9 4.9 %collective-permute-start.1 = (bf16[272,128]{1,0:T(8,128)(2,1)}, bf16[272,128]{1,0:T(8,128)(2,1)S(1)}, u32[]{:S(2)}, u32[]{:S(2)}) collective-permute-start(bf16[272,128]{1,0:T(8,128)(2,1)} %get-tuple-element.16), channel_id=1, source_target_pairs={{0,96},{4,100},{8,104},{12,108},{16,112},{20,116},{24,120},{28,124... | collective-permute-start | bytes 208904 | tf_op jit(solution)/shard_map/ppermute | solution.py:329
  59.4 1.0 collective-permute-start.3
  60.4 1.0 collective-permute-done.1.a_ref
  61.4 3.6 %collective-permute-done.2.b_ref = bf16[272,128]{1,0:T(8,128)(2,1)S(1)} collective-permute-done((bf16[272,128]{1,0:T(8,128)(2,1)}, bf16[272,128]{1,0:T(8,128)(2,1)S(1)}, u32[]{:S(2)}, u32[]{:S(2)}) %collective-permute-start.2) | collective-permute-done | bytes 69664 | tf_op jit(solution)/shard_map/ppermute | solution.py:329
  65.0 0.7 collective-permute-done.3.c_ref
  66.3 2.6 %start_states.1 = bf16[8,128,128]{2,1,0:T(8,128)(2,1)} custom-call(s32[1]{0:T(128)} %bitcast.2.y_ref, bf16[272,128]{1,0:T(8,128)(2,1)} %copy-done.1, bf16[272,128]{1,0:T(8,128)(2,1)} %copy-done.2, bf16[272,128]{1,0:T(8,128)(2,1)} %copy-done.3, f32[8,128,256]{2,1,0:T(8,128)} %get-tuple-element.17.pre_ref, f32[8,8,128]{2,1,0:T(8,128)} %get-tuple-element.18.g_ref), custom_call_target="tpu_custom_call" | custom-call | tf_op jit(solution)/shard_map/start_states/pallas_call | solution.py:247
  68.9 3.4 %all-to-all-start.1 = ((bf16[8,128,128]{2,1,0:T(8,128)(2,1)}), bf16[8,128,128]{2,1,0:T(8,128)(2,1)S(1)}, u32[]{:S(2)}, u32[]{:S(2)}) async-start(bf16[8,128,128]{2,1,0:T(8,128)(2,1)} %start_states.1), calls=%async_computation.1 | async-start | bytes 524288 | tf_op jit(solution)/shard_map/all_to_all | solution.py:332
  72.4 7.4 %all-to-all-done.1.s_ref = bf16[8,128,128]{2,1,0:T(8,128)(2,1)S(1)} async-done(((bf16[8,128,128]{2,1,0:T(8,128)(2,1)}), bf16[8,128,128]{2,1,0:T(8,128)(2,1)S(1)}, u32[]{:S(2)}, u32[]{:S(2)}) %all-to-all-start.1) | async-done | bytes 262176 | tf_op jit(solution)/shard_map/all_to_all | solution.py:332
  79.8 0.7 copy-done
  80.5 5.1 %hidden_part.1 = (bf16[512,1024]{1,0:T(8,128)(2,1)}, bf16[512,512]{1,0:T(8,128)(2,1)}) custom-call(s32[1]{0:T(128)} %bitcast.1.col_ref, f32[512,1024]{1,0:T(8,128)} %get-tuple-element.13.o_ref, bf16[512,1024]{1,0:T(8,128)(2,1)} %get-tuple-element.14.qe_ref, bf16[8,128,128]{2,1,0:T(8,128)(2,1)} %copy-done, bf16[512,1024]{1,0:T(8,128)(2,1)} %gate_ref.1, ...), custom_call_target="tpu_custom_call" | custom-call | tf_op jit(solution)/shard_map/hidden_part/pallas_call | solution.py:271
  85.6 3.0 %part.4 = bf16[512,512]{1,0:T(8,128)(2,1)} custom-call(s32[1]{0:T(128)} %bitcast.4.col_ref, bf16[512,1024]{1,0:T(8,128)(2,1)} %get-tuple-element.19.hid_ref, bf16[1024,2048]{1,0:T(8,128)(2,1)} %w_ref.7), custom_call_target="tpu_custom_call" | custom-call | tf_op jit(solution)/shard_map/part/pallas_call | solution.py:298
  88.6 1.9 %collective-permute-start.4 = (bf16[512,512]{1,0:T(8,128)(2,1)}, bf16[512,512]{1,0:T(8,128)(2,1)S(1)}, u32[]{:S(2)}, u32[]{:S(2)}) collective-permute-start(bf16[512,512]{1,0:T(8,128)(2,1)} %part.4), channel_id=1, source_target_pairs={{0,1},{1,2},{2,3},{3,0},{4,5},{5,6},{6,7},{7,4},{8,9},{9,10},{10,1... | collective-permute-start | bytes 1572872 | tf_op jit(solution)/shard_map/ppermute | solution.py:337
  90.6 3.1 %part.5 = bf16[512,512]{1,0:T(8,128)(2,1)} custom-call(s32[1]{0:T(128)} %bitcast.5.col_ref, bf16[512,1024]{1,0:T(8,128)(2,1)} %get-tuple-element.19.hid_ref, bf16[1024,2048]{1,0:T(8,128)(2,1)} %w_ref.7), custom_call_target="tpu_custom_call" | custom-call | tf_op jit(solution)/shard_map/part/pallas_call | solution.py:298
  93.7 3.0 %collective-permute-start.5 = (bf16[512,512]{1,0:T(8,128)(2,1)S(1)}, bf16[512,512]{1,0:T(8,128)(2,1)S(1)}, u32[]{:S(2)}, u32[]{:S(2)}) collective-permute-start(bf16[512,512]{1,0:T(8,128)(2,1)S(1)} %copy-done.5), channel_id=1, source_target_pairs={{0,2},{1,3},{2,0},{3,1},{4,6},{5,7},{6,4},{7,5},{8,10},{9,11},{10,... | collective-permute-start | bytes 1572872 | tf_op jit(solution)/shard_map/ppermute | solution.py:336
  96.7 3.0 %part.3 = bf16[512,512]{1,0:T(8,128)(2,1)} custom-call(s32[1]{0:T(128)} %bitcast.col_ref, bf16[512,1024]{1,0:T(8,128)(2,1)} %get-tuple-element.19.hid_ref, bf16[1024,2048]{1,0:T(8,128)(2,1)} %w_ref.7), custom_call_target="tpu_custom_call" | custom-call | tf_op jit(solution)/shard_map/part/pallas_call | solution.py:298
  99.7 13.2 %collective-permute-done.4 = bf16[512,512]{1,0:T(8,128)(2,1)S(1)} collective-permute-done((bf16[512,512]{1,0:T(8,128)(2,1)}, bf16[512,512]{1,0:T(8,128)(2,1)S(1)}, u32[]{:S(2)}, u32[]{:S(2)}) %collective-permute-start.4) | collective-permute-done | bytes 524320 | tf_op jit(solution)/shard_map/ppermute | solution.py:337
  113.0 6.2 %collective-permute-done.5 = bf16[512,512]{1,0:T(8,128)(2,1)S(1)} collective-permute-done((bf16[512,512]{1,0:T(8,128)(2,1)S(1)}, bf16[512,512]{1,0:T(8,128)(2,1)S(1)}, u32[]{:S(2)}, u32[]{:S(2)}) %collective-permute-start.5) | collective-permute-done | bytes 524320 | tf_op jit(solution)/shard_map/ppermute | solution.py:336
  119.1 2.1 %add_convert_fusion = bf16[512,512]{1,0:T(8,128)(2,1)} fusion(bf16[512,512]{1,0:T(8,128)(2,1)S(1)} %collective-permute-done.6, bf16[512,512]{1,0:T(8,128)(2,1)S(1)} %collective-permute-done.5, bf16[512,512]{1,0:T(8,128)(2,1)S(1)} %collective-permute-done.4, bf16[512,512]{1,0:T(8,128)(2,1)} %part.3), kind=kLoop, calls=%fused_computation | loop fusion | flops 2097152 | bytes 2621440 | tf_op jit(solution)/shard_map/convert_element_type | solution.py:341
  (17 shorter events, 3.4 us)
Async XLA Ops:
  2.1 2.6 %collective-permute-start = (bf16[8,2048]{1,0:T(8,128)(2,1)S(1)}, bf16[8,2048]{1,0:T(8,128)(2,1)S(1)}, u32[]{:S(2)}, u32[]{:S(2)}) collective-permute-start(bf16[8,2048]{1,0:T(8,128)(2,1)S(1)} %pad_maximum_fusion), channel_id=1, source_target_pairs={{0,4},{4,8},{8,12},{12,16},{16,20},{20,24},{24,28},{28,32},{32,36}... | collective-permute-start | bytes 98312 | tf_op jit(solution)/shard_map/ppermute | solution.py:322
  4.7 0.6 copy-start.4
  53.9 7.5 %collective-permute-start.1 = (bf16[272,128]{1,0:T(8,128)(2,1)}, bf16[272,128]{1,0:T(8,128)(2,1)S(1)}, u32[]{:S(2)}, u32[]{:S(2)}) collective-permute-start(bf16[272,128]{1,0:T(8,128)(2,1)} %get-tuple-element.16), channel_id=1, source_target_pairs={{0,96},{4,100},{8,104},{12,108},{16,112},{20,116},{24,120},{28,124... | collective-permute-start | bytes 208904 | tf_op jit(solution)/shard_map/ppermute | solution.py:329
  58.8 6.2 %collective-permute-start.2 = (bf16[272,128]{1,0:T(8,128)(2,1)}, bf16[272,128]{1,0:T(8,128)(2,1)S(1)}, u32[]{:S(2)}, u32[]{:S(2)}) collective-permute-start(bf16[272,128]{1,0:T(8,128)(2,1)} %get-tuple-element.16), channel_id=1, source_target_pairs={{0,64},{4,68},{8,72},{12,76},{16,80},{20,84},{24,88},{28,92},{32,9... | collective-permute-start | bytes 208904 | tf_op jit(solution)/shard_map/ppermute | solution.py:329
  59.4 6.3 %collective-permute-start.3 = (bf16[272,128]{1,0:T(8,128)(2,1)}, bf16[272,128]{1,0:T(8,128)(2,1)S(1)}, u32[]{:S(2)}, u32[]{:S(2)}) collective-permute-start(bf16[272,128]{1,0:T(8,128)(2,1)} %get-tuple-element.16), channel_id=1, source_target_pairs={{0,32},{4,36},{8,40},{12,44},{16,48},{20,52},{24,56},{28,60},{32,6... | collective-permute-start | bytes 208904 | tf_op jit(solution)/shard_map/ppermute | solution.py:329
  61.4 4.3 %copy-start.1 = (bf16[272,128]{1,0:T(8,128)(2,1)}, bf16[272,128]{1,0:T(8,128)(2,1)S(1)}, u32[]{:S(2)}) copy-start(bf16[272,128]{1,0:T(8,128)(2,1)S(1)} %collective-permute-done.1.a_ref) | copy-start | bytes 208900
  65.0 0.8 copy-start.2
  65.7 0.6 copy-start.3
  68.9 10.9 %all-to-all-start.1 = ((bf16[8,128,128]{2,1,0:T(8,128)(2,1)}), bf16[8,128,128]{2,1,0:T(8,128)(2,1)S(1)}, u32[]{:S(2)}, u32[]{:S(2)}) async-start(bf16[8,128,128]{2,1,0:T(8,128)(2,1)} %start_states.1), calls=%async_computation.1 | async-start | bytes 524288 | tf_op jit(solution)/shard_map/all_to_all | solution.py:332
  79.8 0.7 copy-start
  88.6 5.1 %copy-start.5 = (bf16[512,512]{1,0:T(8,128)(2,1)S(1)}, bf16[512,512]{1,0:T(8,128)(2,1)}, u32[]{:S(2)}) copy-start(bf16[512,512]{1,0:T(8,128)(2,1)} %get-tuple-element.20) | copy-start | bytes 1572868
  88.6 24.3 %collective-permute-start.4 = (bf16[512,512]{1,0:T(8,128)(2,1)}, bf16[512,512]{1,0:T(8,128)(2,1)S(1)}, u32[]{:S(2)}, u32[]{:S(2)}) collective-permute-start(bf16[512,512]{1,0:T(8,128)(2,1)} %part.4), channel_id=1, source_target_pairs={{0,1},{1,2},{2,3},{3,0},{4,5},{5,6},{6,7},{7,4},{8,9},{9,10},{10,1... | collective-permute-start | bytes 1572872 | tf_op jit(solution)/shard_map/ppermute | solution.py:337
  93.6 19.3 %collective-permute-start.6 = (bf16[512,512]{1,0:T(8,128)(2,1)}, bf16[512,512]{1,0:T(8,128)(2,1)S(1)}, u32[]{:S(2)}, u32[]{:S(2)}) collective-permute-start(bf16[512,512]{1,0:T(8,128)(2,1)} %part.5), channel_id=1, source_target_pairs={{0,3},{1,0},{2,1},{3,2},{4,7},{5,4},{6,5},{7,6},{8,11},{9,8},{10,9... | collective-permute-start | bytes 1572872 | tf_op jit(solution)/shard_map/ppermute | solution.py:338
  93.7 25.4 %collective-permute-start.5 = (bf16[512,512]{1,0:T(8,128)(2,1)S(1)}, bf16[512,512]{1,0:T(8,128)(2,1)S(1)}, u32[]{:S(2)}, u32[]{:S(2)}) collective-permute-start(bf16[512,512]{1,0:T(8,128)(2,1)S(1)} %copy-done.5), channel_id=1, source_target_pairs={{0,2},{1,3},{2,0},{3,1},{4,6},{5,7},{6,4},{7,5},{8,10},{9,11},{10,... | collective-permute-start | bytes 1572872 | tf_op jit(solution)/shard_map/ppermute | solution.py:336

commit v2 on v1

v2 whole, which is shorter than its diff:
```python
import functools

import jax
import jax.numpy as jnp
from jax import lax
from jax.experimental import pallas as pl
from jax.experimental.pallas import tpu as pltpu
from jax.sharding import PartitionSpec as P

DK = 128
DV = 128
CHUNK = 128
ROW = 8
EXTRA = 16
SUB = 16
GROUP = 16

f32 = jnp.float32
bf16 = jnp.bfloat16
highest = lax.Precision.HIGHEST


def mm(a, b, dims=((1,), (0,))):
    return lax.dot_general(a, b, (dims, ((), ())), preferred_element_type=f32)


def mm_exact(a, b, dims=((1,), (0,))):
    return lax.dot_general(a, b, (dims, ((), ())), preferred_element_type=f32, precision=highest)


NT = ((1,), (1,))
TN = ((0,), (0,))


SMEM_SPEC = pl.BlockSpec(memory_space=pltpu.SMEM)
VMEM_SPEC = pl.BlockSpec(memory_space=pltpu.VMEM)


def params(mib):
    return pltpu.CompilerParams(vmem_limit_bytes=mib * 1024 * 1024)


def local(x):
    return pltpu.with_memory_space_constraint(x, pltpu.MemorySpace.VMEM)


def far(x):
    return pltpu.with_memory_space_constraint(x, pltpu.MemorySpace.HBM)


def silu(x):
    return x / (1.0 + jnp.exp(-x))


def split3(x):
    hi = x.astype(bf16)
    rest = x - hi.astype(f32)
    mid = rest.astype(bf16)
    low = (rest - mid.astype(f32)).astype(bf16)
    return hi, mid, low


def extras(row):
    full = jnp.broadcast_to(row, (EXTRA, row.shape[1]))
    at = lax.broadcasted_iota(jnp.int32, full.shape, 0)
    hi, mid, low = (part.astype(f32) for part in split3(full))
    return jnp.where(at == 0, hi, jnp.where(at == 1, mid, jnp.where(at == 2, low, 0.0))).astype(bf16)


def tails_kernel(q_ref, k_ref, v_ref, out_ref):
    qw = q_ref.shape[1]
    out_ref[:, 0:qw] = q_ref[...]
    out_ref[:, qw : 2 * qw] = k_ref[...]
    out_ref[:, 2 * qw :] = v_ref[...]


def tails(q, k, v):
    last = q.shape[0] // 8 - 1
    spec = lambda a: pl.BlockSpec((8, a.shape[1]), lambda i: (last, 0))
    width = q.shape[1] + k.shape[1] + v.shape[1]
    return pl.pallas_call(
        tails_kernel,
        grid=(1,),
        in_specs=[spec(q), spec(k), spec(v)],
        out_specs=VMEM_SPEC,
        out_shape=pltpu.VMEM((8, width), bf16),
        name="tails",
    )(q, k, v)


def tile_of(t, q_ref, k_ref, v_ref):
    col, qw = t * 128, q_ref.shape[1]
    if col < qw:
        return q_ref, col
    if col < 2 * qw:
        return k_ref, col - qw
    return v_ref, col - 2 * qw


def load_taps(taps, cq_ref, ck_ref, cv_ref):
    for t in range(taps.shape[0] // 4):
        src, at = tile_of(t, cq_ref, ck_ref, cv_ref)
        w = src[:, at : at + 128].astype(f32)
        for j in range(4):
            taps[t * 4 + j] = jnp.broadcast_to(w[j : j + 1, :], (8, 128))


def conv_tile(pad, taps, tile, key_heads, put):
    stride = CHUNK // 8
    w = [taps[tile * 4 + j] for j in range(4)]
    x = [pad[tile, pl.ds(8 + v, 8, stride=stride), :] for v in range(-3, stride)]
    for v in range(stride):
        y = silu(w[0] * x[v] + w[1] * x[v + 1] + w[2] * x[v + 2] + w[3] * x[v + 3])
        if tile < 2 * key_heads:
            scale = DK ** (-0.5) if tile < key_heads else 1.0
            y = y * (lax.rsqrt(jnp.sum(y * y, -1, keepdims=True) + 1e-06) * scale)
        put(pl.ds(v, 8, stride=stride), y)


def acts_kernel(*refs):
    hbm, (out_ref, taps, pad, done), local_refs, sem = refs[:6], refs[6:10], refs[10:16], refs[16]
    fetches = [pltpu.make_async_copy(a, b, sem.at[n]) for n, (a, b) in enumerate(zip(hbm, local_refs))]
    for fetch in fetches:
        fetch.start()
    for fetch in fetches:
        fetch.wait()
    q_ref, k_ref, v_ref, cq_ref, ck_ref, cv_ref = local_refs
    tokens, qw = q_ref.shape
    c = CHUNK
    tiles = pad.shape[0]
    key_heads = qw // DK
    load_taps(taps, cq_ref, ck_ref, cv_ref)
    for t in range(tiles):
        src, at = tile_of(t, q_ref, k_ref, v_ref)
        raw = src[0:c, at : at + 128]
        out_ref[t, 0:c, :] = raw
        pad[t, 0:8, :] = raw[c - 8 :, :].astype(f32)

    def chunk(b, unused):
        rows = pl.ds(pl.multiple_of(b * c, c), c)
        for t in range(tiles):
            src, at = tile_of(t, q_ref, k_ref, v_ref)
            pad[t, 8 : 8 + c, :] = src[rows, at : at + 128].astype(f32)
        for t in range(tiles):

            def put(where, y):
                done[t, where, :] = y

            conv_tile(pad, taps, t, key_heads, put)
        for t in range(tiles):
            out_ref[t, rows, :] = done[t].astype(bf16)
            pad[t, 0:8, :] = pad[t, c : c + 8, :]
        return unused

    lax.fori_loop(1, tokens // c, chunk, 0)


def acts(q, k, v, cq, ck, cv):
    tokens = q.shape[0]
    tiles = (2 * q.shape[1] + v.shape[1]) // 128
    return pl.pallas_call(
        acts_kernel,
        in_specs=[pl.BlockSpec(memory_space=pl.ANY)] * 6,
        out_shape=[pltpu.VMEM((tiles, tokens, 128), bf16), pltpu.VMEM((tiles * 4, 8, 128), f32)],
        scratch_shapes=[
            pltpu.VMEM((tiles, CHUNK + 8, 128), f32),
            pltpu.VMEM((tiles, CHUNK, 128), f32),
        ]
        + [pltpu.VMEM(x.shape, x.dtype) for x in (q, k, v, cq, ck, cv)]
        + [pltpu.SemaphoreType.DMA((6,))],
        compiler_params=params(12),
        name="acts",
    )(*(far(x) for x in (q, k, v, cq, ck, cv)))


def prep_kernel(
    act_ref, taps, rim_ref, dl_ref, wb_ref,
    o_ref, qe_ref, x_ref,
    pad, fresh0, act0, cols, crow, lm, tm, qa, ke, kt, bv, gams, els, yb, fb, zt, gs,
):
    tiles, tokens, _ = act_ref.shape
    heads = dl_ref.shape[0]
    key_heads = (tiles - heads) // 2
    ratio = heads // key_heads
    c = CHUNK
    ii = lax.broadcasted_iota(jnp.int32, (c, c), 0)
    jj = lax.broadcasted_iota(jnp.int32, (c, c), 1)
    xor = jnp.where(ii >= jj, ii ^ jj, -1)
    lower = (ii >= jj).astype(f32)
    upper = (ii <= jj).astype(f32)
    eye = (ii == jj).astype(f32)
    ones = jnp.ones((c, c), f32)
    ri = lax.broadcasted_iota(jnp.int32, (SUB, c), 0)
    ci = lax.broadcasted_iota(jnp.int32, (SUB, c), 1)
    cx = jnp.where(ri >= ci % SUB, ri ^ (ci % SUB), -1)
    band16 = [(ci // SUB == b).astype(f32).astype(bf16) for b in range(c // SUB)]
    zt[...] = jnp.zeros_like(zt)
    gs[...] = jnp.zeros_like(gs)

    for t in range(tiles):
        pad[t, 0:8, :] = rim_ref[:, t * 128 : t * 128 + 128].astype(f32)
        pad[t, 8 : 8 + c, :] = act_ref[t, 0:c, :].astype(f32)
    for t in range(tiles):

        def put(where, y):
            fresh0[t, where, :] = y

        conv_tile(pad, taps, t, key_heads, put)
    for t in range(tiles):
        act0[t] = fresh0[t].astype(bf16)
    for b in range(tokens // c):
        rows = slice(b * c, (b + 1) * c)
        dl = dl_ref[:, rows]
        crow[b] = mm_exact(dl, upper)
        l_row = mm_exact(dl, ones)
        c_col = mm_exact(lower, dl, NT)
        b_col = mm_exact(eye, wb_ref[:, rows], NT)
        ec = jnp.exp(c_col)
        for n, x in enumerate((c_col, b_col, ec, b_col * ec, jnp.exp(c_col[c - 1 : c, :] - c_col))):
            cols[b, n] = x
        gams[b] = jnp.exp(gs[...])
        els[b] = jnp.exp(l_row)
        gs[...] = gs[...] + l_row

    def expand(part):
        return jnp.concatenate([part * m for m in band16], 0)

    def halves(s):
        return [(i, i + s) for i in range(s, c, 2 * s)]

    def mixing(b, act, rows):
        c_row = crow[b]
        c_col, b_col, ec, be, tail = (cols[b, n] for n in range(5))
        for kh in range(key_heads):
            qb = act[kh, rows, :]
            kb = act[key_heads + kh, rows, :]
            q = qb.astype(f32)
            k = kb.astype(f32)
            gram = mm(kb, kb, NT)
            qk = mm(qb, kb, NT)
            for r in range(ratio):
                h = kh * ratio + r
                at = b * heads + h
                diff = c_col[:, h : h + 1] - c_row[h : h + 1, :]
                spread = jnp.exp(jnp.where(xor >= 0, diff, -1e30))
                beta = b_col[:, h : h + 1]
                lm[at] = (beta * gram * spread).astype(bf16)
                qa[at, :, 0:DK] = (ec[:, h : h + 1] * q).astype(bf16)
                qa[at, :, DK : DK + c] = (qk * spread).astype(bf16)
                ke[at] = (be[:, h : h + 1] * k).astype(bf16)
                kt[at] = (tail[:, h : h + 1] * k).astype(bf16)
                bv[at] = (beta * act[2 * key_heads + h, rows, :].astype(f32)).astype(bf16)

    def later(b, unused):
        mixing(b, act_ref, pl.ds(pl.multiple_of(b * c, c), c))
        return unused

    mixing(0, act0, slice(0, c))
    lax.fori_loop(1, tokens // c, later, 0)

    def flag(m):
        return m.astype(f32).astype(bf16)

    base16 = flag(cx == 0)
    pick16 = {s: flag((cx >= s) & (cx < 2 * s)) for s in (1, 2, 4, 8)}
    pick_rows = {}
    for s in (16, 32, 64):
        part = jnp.concatenate([xor[i:j] for i, j in halves(s)], 0)
        pick_rows[s] = flag((part >= s) & (part < 2 * s))

    def paired(left, right):
        out = []
        for n in range(0, GROUP, 2):
            both = mm(
                jnp.concatenate([left[n], left[n + 1]], 0),
                jnp.concatenate([expand(right[n]), expand(right[n + 1])], 1),
            ).astype(bf16)
            out += [both[0:SUB, 0:c], both[SUB : 2 * SUB, c : 2 * c]]
        return out

    def invert(g, unused):
        group = [g * GROUP + n for n in range(GROUP)]
        small = []
        for h in group:
            lc = lm[h, 0:SUB, :] * band16[0]
            for b in range(1, c // SUB):
                lc = lc + lm[h, b * SUB : (b + 1) * SUB, :] * band16[b]
            small.append(lc)
        tc = [base16 - lc * pick16[1] for lc in small]
        s = 2
        while s < SUB:
            rc = paired([lc * pick16[s] for lc in small], tc)
            fix = paired(tc, rc)
            tc = [tc[n] - fix[n] for n in range(GROUP)]
            s *= 2
        for n, h in enumerate(group):
            tm[h] = expand(tc[n])
        while s < c:
            half = halves(s)
            zero = jnp.zeros((s, c), bf16)
            rr = []
            for h in group:
                sub = jnp.concatenate([lm[h, i:j, :] for i, j in half], 0)
                rr.append(mm(sub * pick_rows[s], tm[h]).astype(bf16))
            for r, h in zip(rr, group):
                full = []
                for n in range(len(half)):
                    full += [zero, r[n * s : (n + 1) * s]]
                sub = jnp.concatenate([tm[h, i:j, :] for i, j in half], 0)
                sub = sub - mm(sub, jnp.concatenate(full, 0)).astype(bf16)
                for n, (i, j) in enumerate(half):
                    tm[h, i:j, :] = sub[n * s : (n + 1) * s]
            s *= 2
        return unused

    lax.fori_loop(0, tokens // c * heads // GROUP, invert, 0)

    def chunk(b, unused):
        rows = pl.ds(pl.multiple_of(b * c, c), c)
        gam = gams[b]
        el = els[b]
        for h in range(heads):
            at = b * heads + h
            kef = ke[at]
            y = mm(kef, zt[h].astype(bf16))
            yb[h, :, 0:DV] = (bv[at].astype(f32) - y[:, :DV]).astype(bf16)
            yb[h, :, DV:] = (gam[h : h + 1, :] * kef.astype(f32) - y[:, DV:]).astype(bf16)
        for h in range(heads):
            fb[h] = mm(tm[b * heads + h], yb[h]).astype(bf16)
        for h in range(heads):
            at = b * heads + h
            z = zt[h]
            fresh = fb[h]
            both = jnp.concatenate([z.astype(bf16), fresh], 0)
            out = mm(qa[at], both)
            o_ref[rows, h * DV : (h + 1) * DV] = out[:, :DV].astype(bf16)
            qe_ref[rows, h * DK : (h + 1) * DK] = (
                gam[h : h + 1, :] * qa[at, :, 0:DK].astype(f32) - out[:, DV:]
            ).astype(bf16)
            scale = el[h : h + 1, :]
            zt[h] = jnp.concatenate([scale, scale], 1) * z + mm(kt[at], fresh, TN)
        return unused

    lax.fori_loop(0, tokens // c, chunk, 0)
    for h in range(heads):
        z = zt[h]
        x_ref[h, 0:DK, :] = z[:, :DV].astype(bf16)
        x_ref[h, DK : 2 * DK, :] = z[:, DV:].astype(bf16)
        x_ref[h, 2 * DK : 2 * DK + EXTRA, :] = extras(gs[h : h + 1, :])


def prep(act, taps, rim, dl, wb):
    tiles, tokens, _ = act.shape
    h = dl.shape[0]
    vw = h * DV
    c = CHUNK
    n = tokens // c
    return pl.pallas_call(
        prep_kernel,
        in_specs=[VMEM_SPEC] * 5,
        out_shape=(
            pltpu.VMEM((tokens, vw), bf16),
            pltpu.VMEM((tokens, h * DK), bf16),
            pltpu.HBM((h, 2 * DK + EXTRA, DV), bf16),
        ),
        scratch_shapes=[
            pltpu.VMEM((tiles, c + 8, 128), f32),
            pltpu.VMEM((tiles, c, 128), f32),
            pltpu.VMEM((tiles, c, 128), bf16),
            pltpu.VMEM((n, 5, c, h), f32),
            pltpu.VMEM((n, h, 128), f32),
            pltpu.VMEM((n * h, c, c), bf16),
            pltpu.VMEM((n * h, c, c), bf16),
            pltpu.VMEM((n * h, c, DK + c), bf16),
            pltpu.VMEM((n * h, c, DK), bf16),
            pltpu.VMEM((n * h, c, DK), bf16),
            pltpu.VMEM((n * h, c, DV), bf16),
            pltpu.VMEM((n, h, 128), f32),
            pltpu.VMEM((n, h, 128), f32),
            pltpu.VMEM((h, c, DV + DK), bf16),
            pltpu.VMEM((h, c, DV + DK), bf16),
            pltpu.VMEM((h, DK, DV + DK), f32),
            pltpu.VMEM((8, 128), f32),
        ],
        compiler_params=params(24),
        name="prep",
    )(*(local(x) for x in (act, taps, rim, dl, wb)))


def log_decay(ref, at):
    rows = ref[at, 2 * DK : 2 * DK + EXTRA, :].astype(f32)
    return rows[0:1, :] + rows[1:2, :] + rows[2:3, :]


def row_kernel(x_ref, pre_ref, g_ref, out_ref):
    count = x_ref.shape[0]
    z = jnp.zeros((DK, DV + DK), f32)
    g = jnp.zeros((1, DV), f32)
    for i in range(count):
        pre_ref[i] = z.astype(bf16)
        g_ref[i] = jnp.broadcast_to(g, (8, DV))
        step = log_decay(x_ref, i)
        d = x_ref[i, DK : 2 * DK, :]
        scale = jnp.broadcast_to(jnp.exp(step), (DK, DV))
        past = jnp.broadcast_to(jnp.exp(g), (DK, DV))
        add = jnp.concatenate([x_ref[i, 0:DK, :].astype(f32), past * d.astype(f32)], 1)
        z = jnp.concatenate([scale, scale], 1) * z - mm(d, z.astype(bf16)) + add
        g = g + step
    out_ref[0:DK, :] = z[:, :DV].astype(bf16)
    out_ref[DK : 2 * DK, :] = z[:, DV:].astype(bf16)
    out_ref[2 * DK : 2 * DK + EXTRA, :] = extras(g)


def row_prefix(x):
    count = x.shape[0]
    return pl.pallas_call(
        row_kernel,
        out_shape=(
            pltpu.VMEM((count, DK, DV + DK), bf16),
            pltpu.VMEM((count, 8, DV), f32),
            pltpu.VMEM((2 * DK + EXTRA, DV), bf16),
        ),
        compiler_params=params(8),
        name="row_prefix",
    )(x)


def start_kernel(y_ref, a_ref, b_ref, c_ref, pre_ref, g_ref, out_ref):
    count = pre_ref.shape[0]
    s = jnp.zeros((DK, DV), f32)
    y = y_ref[0]
    for back, ref in ((3, a_ref), (2, b_ref), (1, c_ref)):
        rows = ref[2 * DK : 2 * DK + EXTRA, :].astype(f32)
        step = rows[0:1, :] + rows[1:2, :] + rows[2:3, :]
        scale = jnp.broadcast_to(jnp.exp(step), (DK, DV))
        after = scale * s - mm(ref[DK : 2 * DK, :], s.astype(bf16)) + ref[0:DK, :].astype(f32)
        s = jnp.where(y >= back, after, s)
    sb = s.astype(bf16)
    for i in range(count):
        z = pre_ref[i]
        scale = jnp.broadcast_to(jnp.exp(g_ref[i, 0:1, :]), (DK, DV))
        out_ref[i] = (scale * s - mm(z[:, DV:], sb) + z[:, :DV].astype(f32)).astype(bf16)


def start_states(y, a, b, c, pre, g):
    count = pre.shape[0]
    return pl.pallas_call(
        start_kernel,
        in_specs=[SMEM_SPEC] + [VMEM_SPEC] * 5,
        out_shape=pltpu.HBM((count, DK, DV), bf16),
        compiler_params=params(8),
        name="start_states",
    )(y, *(local(x) for x in (a, b, c, pre, g)))


def block(w_ref, z_ref, d):
    width = w_ref.shape[1] // 4
    at = pl.multiple_of(((z_ref[0] + d) & 3) * width, width)
    return w_ref[:, pl.ds(at, width)]


def hide(o_ref, qe_ref, s_ref, gate_ref, gain_ref, hid_ref, half):
    rows = slice(half * hid_ref.shape[0], (half + 1) * hid_ref.shape[0])
    gain = gain_ref[...]
    for h in range(s_ref.shape[0]):
        cols = slice(h * DV, (h + 1) * DV)
        x = o_ref[rows, cols].astype(f32) + mm(qe_ref[rows, cols], s_ref[h])
        x = x * lax.rsqrt(jnp.mean(x * x, -1, keepdims=True) + 1e-06)
        hid_ref[:, cols] = (x * gain * silu(gate_ref[:, cols].astype(f32))).astype(bf16)


def first_kernel(
    z_ref, o_ref, qe_ref, s_ref, gain_ref, gate_ref, w_ref, hid_ref, far_ref, wb_ref, gate_b, gate_a, sem
):
    width = wb_ref.shape[1]
    half = hid_ref.shape[0]
    at = pl.multiple_of(((z_ref[0] + 2) & 3) * width, width)
    fetch_a = pltpu.make_async_copy(gate_ref.at[0:half, :], gate_a, sem.at[0])
    fetch_w = pltpu.make_async_copy(w_ref.at[:, pl.ds(at, width)], wb_ref, sem.at[1])
    fetch_b = pltpu.make_async_copy(gate_ref.at[half : 2 * half, :], gate_b, sem.at[2])
    fetch_a.start()
    fetch_w.start()
    fetch_b.start()
    fetch_a.wait()
    hide(o_ref, qe_ref, s_ref, gate_a, gain_ref, hid_ref, 0)
    fetch_w.wait()
    far_ref[...] = mm(hid_ref[...], wb_ref[...]).astype(bf16)
    fetch_b.wait()


def second_kernel(o_ref, qe_ref, s_ref, gate_ref, gain_ref, wb_ref, hid_ref, far_ref):
    hide(o_ref, qe_ref, s_ref, gate_ref, gain_ref, hid_ref, 1)
    far_ref[...] = mm(hid_ref[...], wb_ref[...]).astype(bf16)


def first_half(z, o, qe, s, gate, gain, w):
    tokens, vw = o.shape
    width = w.shape[1] // 4
    return pl.pallas_call(
        first_kernel,
        in_specs=[SMEM_SPEC] + [VMEM_SPEC] * 4 + [pl.BlockSpec(memory_space=pl.ANY)] * 2,
        out_shape=[
            pltpu.VMEM((tokens // 2, vw), bf16),
            pltpu.VMEM((tokens // 2, width), bf16),
            pltpu.VMEM((vw, width), bf16),
            pltpu.VMEM((tokens // 2, vw), bf16),
        ],
        scratch_shapes=[pltpu.VMEM((tokens // 2, vw), bf16), pltpu.SemaphoreType.DMA((3,))],
        compiler_params=params(8),
        name="first_half",
    )(z, *(local(x) for x in (o, qe, s, gain)), far(gate), far(w))


def second_half(o, qe, s, gate, gain, wb):
    tokens, vw = o.shape
    return pl.pallas_call(
        second_kernel,
        in_specs=[VMEM_SPEC] * 6,
        out_shape=[
            pltpu.VMEM((tokens // 2, vw), bf16),
            pltpu.VMEM((tokens // 2, wb.shape[1]), bf16),
        ],
        compiler_params=params(8),
        name="second_half",
    )(*(local(x) for x in (o, qe, s, gate, gain, wb)))


def block(w_ref, z_ref, d):
    width = w_ref.shape[1] // 4
    at = pl.multiple_of(((z_ref[0] + d) & 3) * width, width)
    return w_ref[:, pl.ds(at, width)]


def parts_kernel(z_ref, a_ref, b_ref, w_ref, *outs, jobs):
    for (half, d), out in zip(jobs, outs):
        out[...] = mm((b_ref if half else a_ref)[...], block(w_ref, z_ref, d)).astype(out.dtype)


def parts(z, hid_a, hid_b, w, jobs, kinds):
    tokens = hid_a.shape[0]
    width = w.shape[1] // 4
    return pl.pallas_call(
        functools.partial(parts_kernel, jobs=jobs),
        in_specs=[SMEM_SPEC] + [VMEM_SPEC] * 3,
        out_shape=[pltpu.VMEM((tokens, width), kind) for kind in kinds],
        compiler_params=params(16),
        name="parts",
    )(z, local(hid_a), local(hid_b), local(w))


def finish_kernel(own_a, near_a, sum_a, own_b, near_b, sum_b, out_ref):
    half = own_a.shape[0]
    for at, group in ((0, (own_a, near_a, sum_a)), (half, (own_b, near_b, sum_b))):
        total = sum(ref[...].astype(f32) for ref in group)
        out_ref[at : at + half, :] = total.astype(bf16)


def finish(*pieces):
    rows, width = pieces[0].shape
    return pl.pallas_call(
        finish_kernel,
        in_specs=[VMEM_SPEC] * 6,
        out_shape=jax.ShapeDtypeStruct((2 * rows, width), bf16),
        compiler_params=params(8),
        name="finish",
    )(*(local(x) for x in pieces))


def body(q, k, v, cq, ck, cv, decay_log, write_beta, gate, gain, out_weight):
    tokens = q.shape[0]
    ctx = lax.axis_size("ctx")
    rows = ctx // ROW
    idx = lax.axis_index("ctx")
    z = lax.axis_index("head")
    rim = lax.ppermute(tails(q, k, v), "ctx", [(i, i + 1) for i in range(ctx - 1)])
    act, taps = acts(q, k, v, cq, ck, cv)
    o, qe, x = prep(act, taps, rim, decay_log, write_beta)
    groups = [[y * ROW + j for j in range(ROW)] for y in range(rows)]
    mine = lax.all_to_all(x, "ctx", 0, 0, axis_index_groups=groups, tiled=True)
    pre, g, whole = row_prefix(mine)

    def from_back(d):
        return lax.ppermute(whole, "ctx", [(i, (i + d * ROW) % ctx) for i in range(ctx)])

    s_mine = start_states((idx // ROW).reshape(1), from_back(3), from_back(2), from_back(1), pre, g)
    s = lax.all_to_all(s_mine, "ctx", 0, 0, axis_index_groups=groups, tiled=True)
    z = z.reshape(1)
    gain = gain.reshape(1, DV)
    ahead = lambda x: lax.ppermute(x, "head", [(i, (i + 1) % 4) for i in range(4)])
    behind = lambda x: lax.ppermute(x, "head", [(i, (i + 3) % 4) for i in range(4)])
    hid_a, far_a, wb, gate_b = first_half(z, o, qe, s, gate, gain, out_weight)
    far_a = ahead(far_a)
    hid_b, far_b = second_half(o, qe, s, gate_b, gain, wb)
    far_b = behind(far_b)
    jobs = ((1, 1), (0, 3), (0, 1), (1, 3))
    near_b, near_a, next_a, next_b = parts(z, hid_a, hid_b, out_weight, jobs, (bf16, bf16, f32, f32))
    near_b, near_a = ahead(near_b), behind(near_a)
    own_a, own_b = parts(z, hid_a, hid_b, out_weight, ((0, 0), (1, 0)), (f32, f32))
    sum_a = ahead((next_a + far_a.astype(f32)).astype(bf16))
    sum_b = behind((next_b + far_b.astype(f32)).astype(bf16))
    return finish(own_a, near_a, sum_a, own_b, near_b, sum_b)


def solution(mesh):
    return jax.shard_map(
        body,
        mesh=mesh,
        in_specs=(
            P("ctx", "head"), P("ctx", "head"), P("ctx", "head"),
            P(None, "head"), P(None, "head"), P(None, "head"),
            P("head", "ctx"), P("head", "ctx"), P("ctx", "head"), P(), P("head", None),
        ),
        out_specs=P("ctx", "head"),
        check_vma=False,
    )
```

time: 122 us -> 84.1 us (0.69)
  Pallas kernels: 47.6 us -> 26.6 us
  waiting for transfers between devices: 33 us -> 21.8 us
  local copies, waits for them, and re-layouts: 4.06 us -> 0.01 us
  other arithmetic: 2.11 us -> 0.15 us
  blocking collectives: 17.8 us -> 16.1 us
  starting transfers between devices: 16.6 us -> 18.3 us
    pallas_call x7 -> x10, Pallas kernels: 47.6 us -> 26.6 us  [the longest x1 12.4 us: prep(): pl.pallas_call(prep_kernel, in_specs=[VMEM_SPEC] * 5, out_shape=(pltpu.VM...]
    ppermute x4 -> x7, waiting for transfers between devices: 20.2 us -> 11.4 us  [the longest x3 8.07 us: body(): lax.ppermute(x, 'head', [(i, (i + 3) % 4) for i in range(4)])]
    ppermute x3, waiting for transfers between devices: 5.34 us -> 2.96 us  [from_back(): lax.ppermute(whole, 'ctx', [(i, (i + d * ROW) % ctx) for i in range(ctx)])]
    ppermute x4 -> x7, starting transfers between devices: 6.73 us -> 8.99 us  [the longest x3 4.54 us: body(): lax.ppermute(x, 'head', [(i, (i + 1) % 4) for i in range(4)])]
    slice x3 -> x0, local copies, waits for them, and re-layouts: 2.11 us -> none  [body(): tails = jnp.concatenate([q[tokens - 8:], k[tokens - 8:], v[tokens - 8:]], 1)]
    convert_element_type x1 -> x2, other arithmetic: 2.1 us -> 0.15 us  [the longest x1 0.07 us: body(): sum_a = ahead((next_a + far_a.astype(f32)).astype(bf16))]
    unnamed x12 -> x8, local copies, waits for them, and re-layouts: 1.95 us -> 0.01 us
    all_to_all x1, blocking collectives: 17.8 us -> 16.1 us  [body(): mine = lax.all_to_all(x, 'ctx', 0, 0, axis_index_groups=groups, tiled=True)]
  transfers between devices with their start and end apart: 8 -> 11, of which waited for: 7 -> 8; matrix products, arithmetic and copies ran while one was open for 0% -> 0% of each run, Pallas kernels for 5% -> 9%
where the time goes in v2:
time: 84.1 us; the launch traced here: 83.1 us
  Pallas kernels  26.6 us (32%)
  waiting for transfers between devices  21.8 us (26%)
  starting transfers between devices  18.3 us (22%)
  blocking collectives  16.1 us (19%)
    all_to_all x1, blocking collectives, body(): mine = lax.all_to_all(x, 'ctx', 0, 0, axis_index_groups=groups, tiled=True)  16.1 us
    pallas_call x1, Pallas kernels, prep(): pl.pallas_call(prep_kernel, in_specs=[VMEM_SPEC] * 5, out_shape=(pltpu.VM...  12.4 us
    ppermute x3, waiting for transfers between devices, body(): lax.ppermute(x, 'head', [(i, (i + 3) % 4) for i in range(4)])  8.07 us
    all_to_all x1, waiting for transfers between devices, body(): lax.all_to_all(s_mine, 'ctx', 0, 0, axis_index_groups=groups, tiled=True)  7.43 us
    ppermute x3, starting transfers between devices, from_back(): lax.ppermute(whole, 'ctx', [(i, (i + d * ROW) % ctx) for i in range(ctx)])  5.86 us
    pallas_call x1, Pallas kernels, acts(): pl.pallas_call(acts_kernel, in_specs=[pl.BlockSpec(memory_space=pl.ANY)]...  4.73 us
    ppermute x3, starting transfers between devices, body(): lax.ppermute(x, 'head', [(i, (i + 1) % 4) for i in range(4)])  4.54 us
    all_to_all x1, starting transfers between devices, body(): lax.all_to_all(s_mine, 'ctx', 0, 0, axis_index_groups=groups, tiled=True)  3.41 us
  transfers between devices with their start and end apart: 11, of which 8 were waited for; matrix products, arithmetic and copies ran while one was open for 0% of the time, Pallas kernels for 9%

profile of v2, /device:TPU:32, one launch (start us, length us, event | category | flops | bytes accessed | tf_op | source)
XLA Modules:
  0.0 83.1 jit_solution(303316195747726599)
XLA Ops:
  0.8 1.9 %collective-permute-start = (bf16[8,2048]{1,0:T(8,128)(2,1)S(1)}, bf16[8,2048]{1,0:T(8,128)(2,1)S(1)}, u32[]{:S(2)}, u32[]{:S(2)}) collective-permute-start(bf16[8,2048]{1,0:T(8,128)(2,1)S(1)} %tails.1), channel_id=1, source_target_pairs={{0,4},{4,8},{8,12},{12,16},{16,20},{20,24},{24,28},{28,32},{32,36}... | collective-permute-start | bytes 98312 | tf_op jit(solution)/shard_map/ppermute | solution.py:575
  2.6 4.7 %acts.1 = (bf16[16,512,128]{2,1,0:T(8,128)(2,1)S(1)}, f32[64,8,128]{2,1,0:T(8,128)S(1)}) custom-call(bf16[512,512]{1,0:T(8,128)(2,1)} %q_ref.1, bf16[512,512]{1,0:T(8,128)(2,1)} %k_ref.1, bf16[512,1024]{1,0:T(8,128)(2,1)} %v_ref.1, bf16[4,512]{1,0:T(4,128)(2,1)} %refs_3_.1, bf16[4,512]{1,0:T(4,128)(2,1)} %refs_4_.1, bf16[4,1024]{1,0:T(4,128)(2,1)} %refs_5_.1), custom_call_target="tpu_custom_call" | custom-call | tf_op jit(solution)/shard_map/acts/pallas_call | solution.py:161
  7.4 12.4 %prep.1 = (bf16[512,1024]{1,0:T(8,128)(2,1)S(1)}, bf16[512,1024]{1,0:T(8,128)(2,1)S(1)}, bf16[8,272,128]{2,1,0:T(8,128)(2,1)}) custom-call(bf16[16,512,128]{2,1,0:T(8,128)(2,1)S(1)} %get-tuple-element.25.act_ref, f32[64,8,128]{2,1,0:T(8,128)S(1)} %get-tuple-element.26.taps, bf16[8,2048]{1,0:T(8,128)(2,1)S(1)} %collective-permute-done.rim_ref, ...), custom_call_target="tpu_custom_call" | custom-call | tf_op jit(solution)/shard_map/prep/pallas_call | solution.py:358
  19.8 16.1 %all_to_all.10.x_ref = bf16[8,272,128]{2,1,0:T(8,128)(2,1)S(1)} all-to-all(bf16[8,272,128]{2,1,0:T(8,128)(2,1)} %get-tuple-element.29), channel_id=1, replica_groups={{0,4,8,12,16,20,24,28},{32,36,40,44,48,52,56,60},{64,68,72,76,80,84,88,..., dimensions={0} | all-to-all | bytes 1114112 | tf_op jit(solution)/shard_map/all_to_all | solution.py:579
  35.9 1.2 %row_prefix.1 = (bf16[8,128,256]{2,1,0:T(8,128)(2,1)S(1)}, f32[8,8,128]{2,1,0:T(8,128)S(1)}, bf16[272,128]{1,0:T(8,128)(2,1)S(1)}) custom-call(bf16[8,272,128]{2,1,0:T(8,128)(2,1)S(1)} %all_to_all.10.x_ref), custom_call_target="tpu_custom_call" | custom-call | tf_op jit(solution)/shard_map/row_prefix/pallas_call | solution.py:416
  37.1 1.6 %collective-permute-start.3 = (bf16[272,128]{1,0:T(8,128)(2,1)S(1)}, bf16[272,128]{1,0:T(8,128)(2,1)S(1)}, u32[]{:S(2)}, u32[]{:S(2)}) collective-permute-start(bf16[272,128]{1,0:T(8,128)(2,1)S(1)} %get-tuple-element.30), channel_id=1, source_target_pairs={{0,32},{4,36},{8,40},{12,44},{16,48},{20,52},{24,56},{28,60},{32,6... | collective-permute-start | bytes 208904 | tf_op jit(solution)/shard_map/ppermute | solution.py:583
  38.7 2.9 %collective-permute-start.2 = (bf16[272,128]{1,0:T(8,128)(2,1)S(1)}, bf16[272,128]{1,0:T(8,128)(2,1)S(1)}, u32[]{:S(2)}, u32[]{:S(2)}) collective-permute-start(bf16[272,128]{1,0:T(8,128)(2,1)S(1)} %get-tuple-element.30), channel_id=1, source_target_pairs={{0,64},{4,68},{8,72},{12,76},{16,80},{20,84},{24,88},{28,92},{32,9... | collective-permute-start | bytes 208904 | tf_op jit(solution)/shard_map/ppermute | solution.py:583
  41.6 1.3 %collective-permute-start.1 = (bf16[272,128]{1,0:T(8,128)(2,1)S(1)}, bf16[272,128]{1,0:T(8,128)(2,1)S(1)}, u32[]{:S(2)}, u32[]{:S(2)}) collective-permute-start(bf16[272,128]{1,0:T(8,128)(2,1)S(1)} %get-tuple-element.30), channel_id=1, source_target_pairs={{0,96},{4,100},{8,104},{12,108},{16,112},{20,116},{24,120},{28,124... | collective-permute-start | bytes 208904 | tf_op jit(solution)/shard_map/ppermute | solution.py:583
  42.9 2.1 %collective-permute-done.2.b_ref = bf16[272,128]{1,0:T(8,128)(2,1)S(1)} collective-permute-done((bf16[272,128]{1,0:T(8,128)(2,1)S(1)}, bf16[272,128]{1,0:T(8,128)(2,1)S(1)}, u32[]{:S(2)}, u32[]{:S(2)}) %collective-permute-start.2) | collective-permute-done | bytes 69664 | tf_op jit(solution)/shard_map/ppermute | solution.py:583
  45.9 1.3 %start_states.1 = bf16[8,128,128]{2,1,0:T(8,128)(2,1)} custom-call(s32[1]{0:T(128)} %bitcast.1.y_ref, bf16[272,128]{1,0:T(8,128)(2,1)S(1)} %collective-permute-done.1.a_ref, bf16[272,128]{1,0:T(8,128)(2,1)S(1)} %collective-permute-done.2.b_ref, bf16[272,128]{1,0:T(8,128)(2,1)S(1)} %collective-permute-done.3.c_ref, ...), custom_call_target="tpu_custom_call" | custom-call | tf_op jit(solution)/shard_map/start_states/pallas_call | solution.py:447
  47.2 3.4 %all-to-all-start.1 = ((bf16[8,128,128]{2,1,0:T(8,128)(2,1)}), bf16[8,128,128]{2,1,0:T(8,128)(2,1)S(1)}, u32[]{:S(2)}, u32[]{:S(2)}) async-start(bf16[8,128,128]{2,1,0:T(8,128)(2,1)} %start_states.1), calls=%async_computation.1 | async-start | bytes 524288 | tf_op jit(solution)/shard_map/all_to_all | solution.py:586
  50.6 7.4 %all-to-all-done.1.s_ref = bf16[8,128,128]{2,1,0:T(8,128)(2,1)S(1)} async-done(((bf16[8,128,128]{2,1,0:T(8,128)(2,1)}), bf16[8,128,128]{2,1,0:T(8,128)(2,1)S(1)}, u32[]{:S(2)}, u32[]{:S(2)}) %all-to-all-start.1) | async-done | bytes 262176 | tf_op jit(solution)/shard_map/all_to_all | solution.py:586
  58.1 2.4 %first_half.1 = (bf16[256,1024]{1,0:T(8,128)(2,1)S(1)}, bf16[256,512]{1,0:T(8,128)(2,1)S(1)}, bf16[1024,512]{1,0:T(8,128)(2,1)S(1)}, bf16[256,1024]{1,0:T(8,128)(2,1)S(1)}) custom-call(s32[1]{0:T(128)} %bitcast.z_ref, bf16[512,1024]{1,0:T(8,128)(2,1)S(1)} %get-tuple-element.27.o_ref, bf16[512,1024]{1,0:T(8,128)(2,1)S(1)} %get-tuple-element.28.qe_ref, ...), custom_call_target="tpu_custom_call" | custom-call | tf_op jit(solution)/shard_map/first_half/pallas_call | solution.py:499
  60.5 2.0 %collective-permute-start.5 = (bf16[256,512]{1,0:T(8,128)(2,1)S(1)}, bf16[256,512]{1,0:T(8,128)(2,1)S(1)}, u32[]{:S(2)}, u32[]{:S(2)}) collective-permute-start(bf16[256,512]{1,0:T(8,128)(2,1)S(1)} %get-tuple-element.40), channel_id=1, source_target_pairs={{0,1},{1,2},{2,3},{3,0},{4,5},{5,6},{6,7},{7,4},{8,9},{9,10},{10,1... | collective-permute-start | bytes 786440 | tf_op jit(solution)/shard_map/ppermute | solution.py:589
  62.5 1.0 %second_half.1 = (bf16[256,1024]{1,0:T(8,128)(2,1)S(1)}, bf16[256,512]{1,0:T(8,128)(2,1)S(1)}) custom-call(bf16[512,1024]{1,0:T(8,128)(2,1)S(1)} %get-tuple-element.27.o_ref, bf16[512,1024]{1,0:T(8,128)(2,1)S(1)} %get-tuple-element.28.qe_ref, bf16[8,128,128]{2,1,0:T(8,128)(2,1)S(1)} %all-to-all-done.1.s_ref, ...), custom_call_target="tpu_custom_call" | custom-call | tf_op jit(solution)/shard_map/second_half/pallas_call | solution.py:516
  63.6 1.2 %parts.3 = (bf16[256,512]{1,0:T(8,128)(2,1)S(1)}, bf16[256,512]{1,0:T(8,128)(2,1)S(1)}, f32[256,512]{1,0:T(8,128)S(1)}, f32[256,512]{1,0:T(8,128)S(1)}) custom-call(s32[1]{0:T(128)} %bitcast.z_ref, bf16[256,1024]{1,0:T(8,128)(2,1)S(1)} %get-tuple-element.33.a_ref, bf16[256,1024]{1,0:T(8,128)(2,1)S(1)} %get-tuple-element.36.b_ref, bf16[1024,2048]{1,0:T(8,128)(2,1)S(1)} %copy-done), custom_call_target="tpu_custom_call" | custom-call | tf_op jit(solution)/shard_map/parts/pallas_call | solution.py:542
  64.9 2.2 %collective-permute-start.4 = (bf16[256,512]{1,0:T(8,128)(2,1)S(1)}, bf16[256,512]{1,0:T(8,128)(2,1)S(1)}, u32[]{:S(2)}, u32[]{:S(2)}) collective-permute-start(bf16[256,512]{1,0:T(8,128)(2,1)S(1)} %get-tuple-element.38), channel_id=1, source_target_pairs={{0,3},{1,0},{2,1},{3,2},{4,7},{5,4},{6,5},{7,6},{8,11},{9,8},{10,9... | collective-permute-start | bytes 786440 | tf_op jit(solution)/shard_map/ppermute | solution.py:590
  67.1 1.8 %collective-permute-done.5 = bf16[256,512]{1,0:T(8,128)(2,1)S(1)} collective-permute-done((bf16[256,512]{1,0:T(8,128)(2,1)S(1)}, bf16[256,512]{1,0:T(8,128)(2,1)S(1)}, u32[]{:S(2)}, u32[]{:S(2)}) %collective-permute-start.5) | collective-permute-done | bytes 262176 | tf_op jit(solution)/shard_map/ppermute | solution.py:589
  69.0 2.6 %collective-permute-start.6 = (bf16[256,512]{1,0:T(8,128)(2,1)S(1)}, bf16[256,512]{1,0:T(8,128)(2,1)S(1)}, u32[]{:S(2)}, u32[]{:S(2)}) collective-permute-start(bf16[256,512]{1,0:T(8,128)(2,1)S(1)} %add_convert_fusion.1), channel_id=1, source_target_pairs={{0,1},{1,2},{2,3},{3,0},{4,5},{5,6},{6,7},{7,4},{8,9},{9,10},{10,1... | collective-permute-start | bytes 786440 | tf_op jit(solution)/shard_map/ppermute | solution.py:589
  71.6 1.1 %collective-permute-done.8 = bf16[256,512]{1,0:T(8,128)(2,1)S(1)} collective-permute-done((bf16[256,512]{1,0:T(8,128)(2,1)S(1)}, bf16[256,512]{1,0:T(8,128)(2,1)S(1)}, u32[]{:S(2)}, u32[]{:S(2)}) %collective-permute-start.8) | collective-permute-done | bytes 262176 | tf_op jit(solution)/shard_map/ppermute | solution.py:590
  73.7 4.6 %collective-permute-done.4.near_a = bf16[256,512]{1,0:T(8,128)(2,1)S(1)} collective-permute-done((bf16[256,512]{1,0:T(8,128)(2,1)S(1)}, bf16[256,512]{1,0:T(8,128)(2,1)S(1)}, u32[]{:S(2)}, u32[]{:S(2)}) %collective-permute-start.4) | collective-permute-done | bytes 262176 | tf_op jit(solution)/shard_map/ppermute | solution.py:590
  78.3 1.5 %collective-permute-done.6.sum_a = bf16[256,512]{1,0:T(8,128)(2,1)S(1)} collective-permute-done((bf16[256,512]{1,0:T(8,128)(2,1)S(1)}, bf16[256,512]{1,0:T(8,128)(2,1)S(1)}, u32[]{:S(2)}, u32[]{:S(2)}) %collective-permute-start.6) | collective-permute-done | bytes 262176 | tf_op jit(solution)/shard_map/ppermute | solution.py:589
  79.9 2.3 %collective-permute-done.9.sum_b = bf16[256,512]{1,0:T(8,128)(2,1)S(1)} collective-permute-done((bf16[256,512]{1,0:T(8,128)(2,1)S(1)}, bf16[256,512]{1,0:T(8,128)(2,1)S(1)}, u32[]{:S(2)}, u32[]{:S(2)}) %collective-permute-start.9) | collective-permute-done | bytes 262176 | tf_op jit(solution)/shard_map/ppermute | solution.py:590
  82.2 0.9 %finish.1 = bf16[512,512]{1,0:T(8,128)(2,1)} custom-call(f32[256,512]{1,0:T(8,128)S(1)} %get-tuple-element.37.own_a, bf16[256,512]{1,0:T(8,128)(2,1)S(1)} %collective-permute-done.4.near_a, bf16[256,512]{1,0:T(8,128)(2,1)S(1)} %collective-permute-done.6.sum_a, f32[256,512]{1,0:T(8,128)S(1)} %get-tuple-element.41.own_b, ...), custom_call_target="tpu_custom_call" | custom-call | tf_op jit(solution)/shard_map/finish/pallas_call | solution.py:560
  (19 shorter events, 2.8 us)
Async XLA Ops:
  0.0 7.4 %copy-start.2 = (f32[8,512]{1,0:T(8,128)S(1)}, f32[8,512]{1,0:T(8,128)}, u32[]{:S(2)}) copy-start(f32[8,512]{1,0:T(8,128)} %wb_ref.1) | copy-start | bytes 49156
  0.0 7.4 %copy-start.1 = (f32[8,512]{1,0:T(8,128)S(1)}, f32[8,512]{1,0:T(8,128)}, u32[]{:S(2)}) copy-start(f32[8,512]{1,0:T(8,128)} %dl_ref.1) | copy-start | bytes 49156
  0.8 57.3 %copy-start.3 = (f32[128]{0:T(128)S(1)}, f32[128]{0:T(128)}, u32[]{:S(2)}) copy-start(f32[128]{0:T(128)} %param.20) | copy-start | bytes 1540
  0.8 6.6 %collective-permute-start = (bf16[8,2048]{1,0:T(8,128)(2,1)S(1)}, bf16[8,2048]{1,0:T(8,128)(2,1)S(1)}, u32[]{:S(2)}, u32[]{:S(2)}) collective-permute-start(bf16[8,2048]{1,0:T(8,128)(2,1)S(1)} %tails.1), channel_id=1, source_target_pairs={{0,4},{4,8},{8,12},{12,16},{16,20},{20,24},{24,28},{28,32},{32,36}... | collective-permute-start | bytes 98312 | tf_op jit(solution)/shard_map/ppermute | solution.py:575
  37.1 5.9 %collective-permute-start.3 = (bf16[272,128]{1,0:T(8,128)(2,1)S(1)}, bf16[272,128]{1,0:T(8,128)(2,1)S(1)}, u32[]{:S(2)}, u32[]{:S(2)}) collective-permute-start(bf16[272,128]{1,0:T(8,128)(2,1)S(1)} %get-tuple-element.30), channel_id=1, source_target_pairs={{0,32},{4,36},{8,40},{12,44},{16,48},{20,52},{24,56},{28,60},{32,6... | collective-permute-start | bytes 208904 | tf_op jit(solution)/shard_map/ppermute | solution.py:583
  38.7 6.4 %collective-permute-start.2 = (bf16[272,128]{1,0:T(8,128)(2,1)S(1)}, bf16[272,128]{1,0:T(8,128)(2,1)S(1)}, u32[]{:S(2)}, u32[]{:S(2)}) collective-permute-start(bf16[272,128]{1,0:T(8,128)(2,1)S(1)} %get-tuple-element.30), channel_id=1, source_target_pairs={{0,64},{4,68},{8,72},{12,76},{16,80},{20,84},{24,88},{28,92},{32,9... | collective-permute-start | bytes 208904 | tf_op jit(solution)/shard_map/ppermute | solution.py:583
  41.6 4.3 %collective-permute-start.1 = (bf16[272,128]{1,0:T(8,128)(2,1)S(1)}, bf16[272,128]{1,0:T(8,128)(2,1)S(1)}, u32[]{:S(2)}, u32[]{:S(2)}) collective-permute-start(bf16[272,128]{1,0:T(8,128)(2,1)S(1)} %get-tuple-element.30), channel_id=1, source_target_pairs={{0,96},{4,100},{8,104},{12,108},{16,112},{20,116},{24,120},{28,124... | collective-permute-start | bytes 208904 | tf_op jit(solution)/shard_map/ppermute | solution.py:583
  47.2 10.9 %all-to-all-start.1 = ((bf16[8,128,128]{2,1,0:T(8,128)(2,1)}), bf16[8,128,128]{2,1,0:T(8,128)(2,1)S(1)}, u32[]{:S(2)}, u32[]{:S(2)}) async-start(bf16[8,128,128]{2,1,0:T(8,128)(2,1)} %start_states.1), calls=%async_computation.1 | async-start | bytes 524288 | tf_op jit(solution)/shard_map/all_to_all | solution.py:586
  58.1 5.6 %copy-start = (bf16[1024,2048]{1,0:T(8,128)(2,1)S(1)}, bf16[1024,2048]{1,0:T(8,128)(2,1)}, u32[]{:S(2)}) copy-start(bf16[1024,2048]{1,0:T(8,128)(2,1)} %w_ref.5) | copy-start | bytes 12582916
  60.5 8.4 %collective-permute-start.5 = (bf16[256,512]{1,0:T(8,128)(2,1)S(1)}, bf16[256,512]{1,0:T(8,128)(2,1)S(1)}, u32[]{:S(2)}, u32[]{:S(2)}) collective-permute-start(bf16[256,512]{1,0:T(8,128)(2,1)S(1)} %get-tuple-element.40), channel_id=1, source_target_pairs={{0,1},{1,2},{2,3},{3,0},{4,5},{5,6},{6,7},{7,4},{8,9},{9,10},{10,1... | collective-permute-start | bytes 786440 | tf_op jit(solution)/shard_map/ppermute | solution.py:589
  63.5 9.2 %collective-permute-start.8 = (bf16[256,512]{1,0:T(8,128)(2,1)S(1)}, bf16[256,512]{1,0:T(8,128)(2,1)S(1)}, u32[]{:S(2)}, u32[]{:S(2)}) collective-permute-start(bf16[256,512]{1,0:T(8,128)(2,1)S(1)} %get-tuple-element.44), channel_id=1, source_target_pairs={{0,3},{1,0},{2,1},{3,2},{4,7},{5,4},{6,5},{7,6},{8,11},{9,8},{10,9... | collective-permute-start | bytes 786440 | tf_op jit(solution)/shard_map/ppermute | solution.py:590
  64.9 13.4 %collective-permute-start.4 = (bf16[256,512]{1,0:T(8,128)(2,1)S(1)}, bf16[256,512]{1,0:T(8,128)(2,1)S(1)}, u32[]{:S(2)}, u32[]{:S(2)}) collective-permute-start(bf16[256,512]{1,0:T(8,128)(2,1)S(1)} %get-tuple-element.38), channel_id=1, source_target_pairs={{0,3},{1,0},{2,1},{3,2},{4,7},{5,4},{6,5},{7,6},{8,11},{9,8},{10,9... | collective-permute-start | bytes 786440 | tf_op jit(solution)/shard_map/ppermute | solution.py:590
  67.1 11.2 %collective-permute-start.7 = (bf16[256,512]{1,0:T(8,128)(2,1)S(1)}, bf16[256,512]{1,0:T(8,128)(2,1)S(1)}, u32[]{:S(2)}, u32[]{:S(2)}) collective-permute-start(bf16[256,512]{1,0:T(8,128)(2,1)S(1)} %get-tuple-element.42), channel_id=1, source_target_pairs={{0,1},{1,2},{2,3},{3,0},{4,5},{5,6},{6,7},{7,4},{8,9},{9,10},{10,1... | collective-permute-start | bytes 786440 | tf_op jit(solution)/shard_map/ppermute | solution.py:589
  69.0 10.8 %collective-permute-start.6 = (bf16[256,512]{1,0:T(8,128)(2,1)S(1)}, bf16[256,512]{1,0:T(8,128)(2,1)S(1)}, u32[]{:S(2)}, u32[]{:S(2)}) collective-permute-start(bf16[256,512]{1,0:T(8,128)(2,1)S(1)} %add_convert_fusion.1), channel_id=1, source_target_pairs={{0,1},{1,2},{2,3},{3,0},{4,5},{5,6},{6,7},{7,4},{8,9},{9,10},{10,1... | collective-permute-start | bytes 786440 | tf_op jit(solution)/shard_map/ppermute | solution.py:589
  72.8 9.4 %collective-permute-start.9 = (bf16[256,512]{1,0:T(8,128)(2,1)S(1)}, bf16[256,512]{1,0:T(8,128)(2,1)S(1)}, u32[]{:S(2)}, u32[]{:S(2)}) collective-permute-start(bf16[256,512]{1,0:T(8,128)(2,1)S(1)} %add_convert_fusion), channel_id=1, source_target_pairs={{0,3},{1,0},{2,1},{3,2},{4,7},{5,4},{6,5},{7,6},{8,11},{9,8},{10,9... | collective-permute-start | bytes 786440 | tf_op jit(solution)/shard_map/ppermute | solution.py:590
